TPU v7x, 512 devices: a whole 4x4x16 slice. The times are simulated.
512 devices in a mesh: line: 32 (over y, x, core), bus: 16 (over z).
Axes of the slice: x: 4, y: 4, z: 16, core: 2. Of those that a mesh axis runs over, the one named last changes fastest.
Arguments:
- ptdf: bfloat16 [8192, 100352], P('line', 'bus')
- base_injection: float32 [100352], P('bus'), may hold values from -6 to 6
- injection_gain: float32 [100352], P('bus'), may hold values from 0.3 to 3
- factor_of_bus: int32 [100352], P('bus'), may hold values from 0 to 511
- line_rating: int32 [8192], P('line'), may hold values from 60 to 300
- directions: int32 [30, 512], replicated, may hold values from 1 to 1073741823, as said below
- shifts: int32 [8, 512], replicated, may hold values from 0 to 1073741823
- chol_factor: float32 [512, 512], replicated
- proposal_mean: float32 [512], replicated, may hold values from -0.3 to 0.3
Outputs:
- flows: float32 [1024, 8192], P('bus', 'line')
- overload: float32 [1024], P('bus')
- weight: float32 [1024], P('bus')
- new_mean: float32 [512], replicated
Inputs may be any that keep to these rules, and one draw needn't show every extreme that they name: directions[b, f] lies in [2^(29 - b), 2^(30 - b)), as Sobol direction numbers do.
All inputs are finite; a program needn't handle non-finite values.
Results may differ from a plain program's by a relative error of at most 0.0029.
Values sent between devices are 32-bit elements; how exact they have to be, the bound alone decides.
A program may use at most 64 MiB of HBM per device.

v0:
```python
import math

import jax
import jax.numpy as jnp
from jax import lax
from jax.sharding import PartitionSpec as P

POINTS = 128


SHARP = 8.0
HIGH = lax.Precision.HIGHEST


def normals(directions, shifts, start_row, row_count):
    scenario = start_row + jnp.arange(row_count, dtype=jnp.int32)
    sobol_point = scenario % POINTS
    shift_index = scenario // POINTS
    digits = jnp.zeros((row_count, directions.shape[1]), jnp.int32)
    for bit_index in range(max(1, (POINTS - 1).bit_length())):
        picked = sobol_point >> bit_index & 1
        digits = digits ^ picked[:, None] * directions[bit_index][None, :]
    chosen = (shift_index[:, None] == jnp.arange(shifts.shape[0], dtype=jnp.int32)[None, :]).astype(
        jnp.int32
    )
    offset = jnp.sum(chosen[:, :, None] * shifts[None, :, :], axis=1)
    digits = digits ^ offset
    uniform = (2 * (digits >> 7) + 1).astype(jnp.float32) / 16777216.0
    return math.sqrt(2.0) * lax.erf_inv(2.0 * uniform - 1.0)


def per_device(
    ptdf,
    base_injection,
    injection_gain,
    factor_of_bus,
    line_rating,
    directions,
    shifts,
    chol_factor,
    proposal_mean,
):
    bus_devices = lax.axis_size("bus")
    lines_total = ptdf.shape[0] * lax.axis_size("line")
    scenarios = POINTS * shifts.shape[0]
    block_rows = scenarios // bus_devices
    own_start = lax.axis_index("bus") * block_rows
    factors = lax.dot_general(
        normals(directions, shifts, 0, scenarios) + proposal_mean[None, :],
        chol_factor,
        (((1,), (1,)), ((), ())),
        precision=HIGH,
        preferred_element_type=jnp.float32,
    )
    rating = line_rating.astype(jnp.float32) * 0.01
    block_size = min(block_rows * lax.axis_size("bus"), 128)

    def one_block(index):
        rows = lax.dynamic_slice_in_dim(factors, index * block_size, block_size, 0)
        picked = jnp.take(rows, factor_of_bus, axis=1)
        injections = (base_injection[None, :] + injection_gain[None, :] * picked).astype(
            jnp.bfloat16
        )
        return lax.dot_general(
            injections, ptdf, (((1,), (1,)), ((), ())), preferred_element_type=jnp.float32
        )

    pieces = lax.map(
        one_block, jnp.arange(block_rows * lax.axis_size("bus") // block_size, dtype=jnp.int32)
    )
    flows = lax.psum_scatter(
        pieces.reshape(block_rows * lax.axis_size("bus"), ptdf.shape[0]),
        "bus",
        scatter_dimension=0,
        tiled=True,
    )
    own_normals = normals(directions, shifts, own_start, block_rows)
    likelihood = jnp.exp(
        -jnp.dot(own_normals, proposal_mean, precision=HIGH, preferred_element_type=jnp.float32)
    )
    share = (
        jnp.sum(jax.nn.softplus(SHARP * (jnp.abs(flows) / rating[None, :] - 1.0)), axis=1)
        / SHARP
        / lines_total
    )
    overload = lax.psum(share, "line")
    emphasis = likelihood * overload
    moved_part = jnp.dot(emphasis, own_normals, precision=HIGH, preferred_element_type=jnp.float32)
    moved, total = lax.psum((moved_part, jnp.sum(emphasis)), "bus")
    weight = scenarios * likelihood * overload / total
    new_mean = proposal_mean + moved / total
    return (flows, overload, weight, new_mean)


def solution(mesh):
    return jax.shard_map(
        per_device,
        mesh=mesh,
        in_specs=(P("line", "bus"), P("bus"), P("bus"), P("bus"), P("line"), P(), P(), P(), P()),
        out_specs=(P("bus", "line"), P("bus"), P("bus"), P()),
        check_vma=False,
    )
```

profile of v0, /device:TPU:1, one launch (start us, length us, event | category | flops | bytes accessed | tf_op | source)
XLA Modules:
  0.0 386.1 jit_solution(3735118935437047624)
XLA Ops:
  7.3 0.2 fusion.115
  7.5 1.0 fusion.158
  8.5 7.0 %multiply_reduce_fusion = s32[1024,512]{1,0:T(8,128)S(1)} fusion(s32[8,512]{1,0:T(8,128)} %param.17, s32[1024,8]{1,0:T(8,128)S(1)} %fusion.115), kind=kLoop, calls=%fused_computation.16 | loop fusion | flops 7864320 | bytes 2146304 | tf_op jit(solution)/shard_map/reduce_sum | solution.py:26
  15.6 9.1 %fusion.11 = f32[1024,512]{0,1:T(8,128)S(1)} fusion(f32[512,512]{1,0:T(8,128)S(1)} %copy-done, s32[1024,512]{1,0:T(8,128)S(1)} %multiply_reduce_fusion, f32[512]{0:T(512)S(1)} %copy-done.3, s32[512]{0:T(512)S(1)} %bitcast.46, s32[1024]{0:T(1024)S(1)} %get-tuple-element.98, s32[512]{0:T(512)S(1)} %bitcast.48, s32[1024]{0:T(1024)S(1)} %get-tuple-element.99, ...), kind=kOutput, calls=%fused_computation.20 | convolution fusion | flops 3252158464 | bytes 5287936 | tf_op jit(solution)/shard_map/dot_general | solution.py:48
  24.7 189.2 %while.10 = (s32[]{:T(128)}, f32[8,128,256]{2,1,0:T(8,128)}, f32[6272]{0:T(1024)S(1)}, f32[6272]{0:T(1024)}, s32[6272]{0:T(1024)S(1)}, /*index=5*/s32[8]{0:T(128...) while((s32[]{:T(128)}, f32[8,128,256]{2,1,0:T(8,128)}, ...), condition=%wide.region_2.3_spmd, body=%wide.region_1.2_spmd.sunk | while | flops 414316672 | bytes 13721023 | solution.py:68
  24.9 0.6 dynamic_slice.11
  26.2 0.1 fusion.168
  26.3 12.6 %gather_fusion = f32[6272,128]{1,0:T(8,128)} fusion(f32[128,512]{0,1:T(8,128)S(1)} %constant_dynamic-slice_fusion.2, s32[7168]{0:T(1024)S(1)} %pad_clamp_fusion.2), kind=kCustom, calls=%fused_computation.clone.1 | custom fusion | bytes 6447616 | tf_op jit(solution)/shard_map/while/body/eval_jaxpr/jit(_take)/gather | solution.py:60
  38.9 9.6 %fusion.169 = f32[8,128,256]{2,1,0:T(8,128)} fusion(f32[8,128,256]{2,1,0:T(8,128)} %get-tuple-element.172, s32[]{:T(128)S(6)} %copy.20, bf16[256,6272]{1,0:T(8,128)(2,1)} %get-tuple-element.190, f32[6272,128]{1,0:T(8,128)} %gather_fusion, f32[6272]{0:T(1024)S(1)} %get-tuple-element.185, f32[6272]{0:T(1024)} %get-tuple-element.186, ...), kind=kOutput, calls=%fused_computation.8.clone.1 | convolution fusion | flops 414253056 | bytes 6613636 | tf_op jit(solution)/shard_map/while/body/eval_jaxpr/dot_general | solution.py:64
  48.5 0.6 dynamic_slice.11
  49.8 0.1 fusion.168
  49.9 12.6 %gather_fusion = f32[6272,128]{1,0:T(8,128)} fusion(f32[128,512]{0,1:T(8,128)S(1)} %constant_dynamic-slice_fusion.2, s32[7168]{0:T(1024)S(1)} %pad_clamp_fusion.2), kind=kCustom, calls=%fused_computation.clone.1 | custom fusion | bytes 6447616 | tf_op jit(solution)/shard_map/while/body/eval_jaxpr/jit(_take)/gather | solution.py:60
  62.5 9.6 %fusion.169 = f32[8,128,256]{2,1,0:T(8,128)} fusion(f32[8,128,256]{2,1,0:T(8,128)} %get-tuple-element.172, s32[]{:T(128)S(6)} %copy.20, bf16[256,6272]{1,0:T(8,128)(2,1)} %get-tuple-element.190, f32[6272,128]{1,0:T(8,128)} %gather_fusion, f32[6272]{0:T(1024)S(1)} %get-tuple-element.185, f32[6272]{0:T(1024)} %get-tuple-element.186, ...), kind=kOutput, calls=%fused_computation.8.clone.1 | convolution fusion | flops 414253056 | bytes 6613636 | tf_op jit(solution)/shard_map/while/body/eval_jaxpr/dot_general | solution.py:64
  72.1 0.6 dynamic_slice.11
  73.4 0.1 fusion.168
  73.5 12.6 %gather_fusion = f32[6272,128]{1,0:T(8,128)} fusion(f32[128,512]{0,1:T(8,128)S(1)} %constant_dynamic-slice_fusion.2, s32[7168]{0:T(1024)S(1)} %pad_clamp_fusion.2), kind=kCustom, calls=%fused_computation.clone.1 | custom fusion | bytes 6447616 | tf_op jit(solution)/shard_map/while/body/eval_jaxpr/jit(_take)/gather | solution.py:60
  86.1 9.6 %fusion.169 = f32[8,128,256]{2,1,0:T(8,128)} fusion(f32[8,128,256]{2,1,0:T(8,128)} %get-tuple-element.172, s32[]{:T(128)S(6)} %copy.20, bf16[256,6272]{1,0:T(8,128)(2,1)} %get-tuple-element.190, f32[6272,128]{1,0:T(8,128)} %gather_fusion, f32[6272]{0:T(1024)S(1)} %get-tuple-element.185, f32[6272]{0:T(1024)} %get-tuple-element.186, ...), kind=kOutput, calls=%fused_computation.8.clone.1 | convolution fusion | flops 414253056 | bytes 6613636 | tf_op jit(solution)/shard_map/while/body/eval_jaxpr/dot_general | solution.py:64
  95.7 0.6 dynamic_slice.11
  97.0 0.1 fusion.168
  97.1 12.6 %gather_fusion = f32[6272,128]{1,0:T(8,128)} fusion(f32[128,512]{0,1:T(8,128)S(1)} %constant_dynamic-slice_fusion.2, s32[7168]{0:T(1024)S(1)} %pad_clamp_fusion.2), kind=kCustom, calls=%fused_computation.clone.1 | custom fusion | bytes 6447616 | tf_op jit(solution)/shard_map/while/body/eval_jaxpr/jit(_take)/gather | solution.py:60
  109.7 9.6 %fusion.169 = f32[8,128,256]{2,1,0:T(8,128)} fusion(f32[8,128,256]{2,1,0:T(8,128)} %get-tuple-element.172, s32[]{:T(128)S(6)} %copy.20, bf16[256,6272]{1,0:T(8,128)(2,1)} %get-tuple-element.190, f32[6272,128]{1,0:T(8,128)} %gather_fusion, f32[6272]{0:T(1024)S(1)} %get-tuple-element.185, f32[6272]{0:T(1024)} %get-tuple-element.186, ...), kind=kOutput, calls=%fused_computation.8.clone.1 | convolution fusion | flops 414253056 | bytes 6613636 | tf_op jit(solution)/shard_map/while/body/eval_jaxpr/dot_general | solution.py:64
  119.4 0.6 dynamic_slice.11
  120.7 0.1 fusion.168
  120.8 12.6 %gather_fusion = f32[6272,128]{1,0:T(8,128)} fusion(f32[128,512]{0,1:T(8,128)S(1)} %constant_dynamic-slice_fusion.2, s32[7168]{0:T(1024)S(1)} %pad_clamp_fusion.2), kind=kCustom, calls=%fused_computation.clone.1 | custom fusion | bytes 6447616 | tf_op jit(solution)/shard_map/while/body/eval_jaxpr/jit(_take)/gather | solution.py:60
  133.4 9.6 %fusion.169 = f32[8,128,256]{2,1,0:T(8,128)} fusion(f32[8,128,256]{2,1,0:T(8,128)} %get-tuple-element.172, s32[]{:T(128)S(6)} %copy.20, bf16[256,6272]{1,0:T(8,128)(2,1)} %get-tuple-element.190, f32[6272,128]{1,0:T(8,128)} %gather_fusion, f32[6272]{0:T(1024)S(1)} %get-tuple-element.185, f32[6272]{0:T(1024)} %get-tuple-element.186, ...), kind=kOutput, calls=%fused_computation.8.clone.1 | convolution fusion | flops 414253056 | bytes 6613636 | tf_op jit(solution)/shard_map/while/body/eval_jaxpr/dot_general | solution.py:64
  143.0 0.6 dynamic_slice.11
  144.3 0.1 fusion.168
  144.4 12.6 %gather_fusion = f32[6272,128]{1,0:T(8,128)} fusion(f32[128,512]{0,1:T(8,128)S(1)} %constant_dynamic-slice_fusion.2, s32[7168]{0:T(1024)S(1)} %pad_clamp_fusion.2), kind=kCustom, calls=%fused_computation.clone.1 | custom fusion | bytes 6447616 | tf_op jit(solution)/shard_map/while/body/eval_jaxpr/jit(_take)/gather | solution.py:60
  157.0 9.6 %fusion.169 = f32[8,128,256]{2,1,0:T(8,128)} fusion(f32[8,128,256]{2,1,0:T(8,128)} %get-tuple-element.172, s32[]{:T(128)S(6)} %copy.20, bf16[256,6272]{1,0:T(8,128)(2,1)} %get-tuple-element.190, f32[6272,128]{1,0:T(8,128)} %gather_fusion, f32[6272]{0:T(1024)S(1)} %get-tuple-element.185, f32[6272]{0:T(1024)} %get-tuple-element.186, ...), kind=kOutput, calls=%fused_computation.8.clone.1 | convolution fusion | flops 414253056 | bytes 6613636 | tf_op jit(solution)/shard_map/while/body/eval_jaxpr/dot_general | solution.py:64
  166.6 0.6 dynamic_slice.11
  167.9 0.1 fusion.168
  168.0 12.6 %gather_fusion = f32[6272,128]{1,0:T(8,128)} fusion(f32[128,512]{0,1:T(8,128)S(1)} %constant_dynamic-slice_fusion.2, s32[7168]{0:T(1024)S(1)} %pad_clamp_fusion.2), kind=kCustom, calls=%fused_computation.clone.1 | custom fusion | bytes 6447616 | tf_op jit(solution)/shard_map/while/body/eval_jaxpr/jit(_take)/gather | solution.py:60
  180.6 9.6 %fusion.169 = f32[8,128,256]{2,1,0:T(8,128)} fusion(f32[8,128,256]{2,1,0:T(8,128)} %get-tuple-element.172, s32[]{:T(128)S(6)} %copy.20, bf16[256,6272]{1,0:T(8,128)(2,1)} %get-tuple-element.190, f32[6272,128]{1,0:T(8,128)} %gather_fusion, f32[6272]{0:T(1024)S(1)} %get-tuple-element.185, f32[6272]{0:T(1024)} %get-tuple-element.186, ...), kind=kOutput, calls=%fused_computation.8.clone.1 | convolution fusion | flops 414253056 | bytes 6613636 | tf_op jit(solution)/shard_map/while/body/eval_jaxpr/dot_general | solution.py:64
  190.3 0.6 dynamic_slice.11
  191.6 0.1 fusion.168
  191.7 12.6 %gather_fusion = f32[6272,128]{1,0:T(8,128)} fusion(f32[128,512]{0,1:T(8,128)S(1)} %constant_dynamic-slice_fusion.2, s32[7168]{0:T(1024)S(1)} %pad_clamp_fusion.2), kind=kCustom, calls=%fused_computation.clone.1 | custom fusion | bytes 6447616 | tf_op jit(solution)/shard_map/while/body/eval_jaxpr/jit(_take)/gather | solution.py:60
  204.3 9.6 %fusion.169 = f32[8,128,256]{2,1,0:T(8,128)} fusion(f32[8,128,256]{2,1,0:T(8,128)} %get-tuple-element.172, s32[]{:T(128)S(6)} %copy.20, bf16[256,6272]{1,0:T(8,128)(2,1)} %get-tuple-element.190, f32[6272,128]{1,0:T(8,128)} %gather_fusion, f32[6272]{0:T(1024)S(1)} %get-tuple-element.185, f32[6272]{0:T(1024)} %get-tuple-element.186, ...), kind=kOutput, calls=%fused_computation.8.clone.1 | convolution fusion | flops 414253056 | bytes 6613636 | tf_op jit(solution)/shard_map/while/body/eval_jaxpr/dot_general | solution.py:64
  214.0 0.1 fusion.120
  214.1 0.4 multiply_reduce_fusion.1
  214.5 0.4 select_multiply_fusion
  214.9 64.8 %reduce-scatter.2.cloned.1.call-done = f32[64,256]{1,0:T(8,128)} async-done(((f32[1024,256]{1,0:T(8,128)}), f32[64,256]{1,0:T(8,128)}) %reduce-scatter.2.cloned.1.call-update) | async-done | bytes 65552 | tf_op jit(solution)/shard_map/reduce_scatter | solution.py:71
  279.7 1.0 fusion.119
  280.7 72.9 %psum.21 = f32[64]{0:T(128)S(1)} all-reduce(f32[64]{0:T(128)S(1)} %broadcast_multiply_fusion), channel_id=1, replica_groups=mesh['line'=32,'bus'=16] {'line'}, use_global_device_ids=true, to_apply=%region_5.6 | all-reduce | flops 64 | bytes 512 | tf_op jit(solution)/shard_map/psum | solution.py:86
  353.6 0.8 multiply_reduce_fusion.2
  354.4 0.2 fusion.126
  354.6 22.2 %all-reduce = (f32[]{:T(128)}, f32[512]{0:T(512)S(1)}) all-reduce(f32[]{:T(128)} %get-tuple-element.96, f32[512]{0:T(512)S(1)} %bitcast.50), channel_id=1, replica_groups=mesh['line'=32,'bus'=16] {'bus'}, use_global_device_ids=true, to_apply=%region_8.9 | all-reduce | flops 513 | bytes 4104 | tf_op jit(solution)/shard_map/psum | solution.py:89
  376.8 1.2 multiply_divide_fusion
  378.0 1.3 divide_add_fusion
  (54 shorter events, 0.7 us)
Async XLA Ops:
  7.2 8.4 %copy-start = (f32[512,512]{1,0:T(8,128)S(1)}, f32[512,512]{1,0:T(8,128)}, u32[]{:S(2)}) copy-start(f32[512,512]{1,0:T(8,128)} %param.18) | copy-start | bytes 3145732
  7.2 8.3 %copy-start.3 = (f32[512]{0:T(512)S(1)}, f32[512]{0:T(512)}, u32[]{:S(2)}) copy-start(f32[512]{0:T(512)} %param.19) | copy-start | bytes 6148
  7.2 272.5 %reduce-scatter.2.cloned.1.call-start = ((), (), s32[]{:S(2)}) async-start(), calls=%async_computation.1 | async-start | bytes 1114112 | tf_op jit(solution)/shard_map/reduce_scatter | solution.py:71
  15.5 9.1 %copy-start.1 = (s32[6272]{0:T(1024)S(1)}, s32[6272]{0:T(1024)}, u32[]{:S(2)}) copy-start(s32[6272]{0:T(1024)} %param.14) | copy-start | bytes 75268
  15.5 9.1 %copy-start.6 = (f32[6272]{0:T(1024)S(1)}, f32[6272]{0:T(1024)}, u32[]{:S(2)}) copy-start(f32[6272]{0:T(1024)} %param.12) | copy-start | bytes 75268
  24.6 189.5 %copy-start.2 = (s32[8,512]{1,0:T(8,128)S(1)}, s32[8,512]{1,0:T(8,128)}, u32[]{:S(2)}) copy-start(s32[8,512]{1,0:T(8,128)} %param.17) | copy-start | bytes 49156
  24.7 189.8 %copy-start.5 = (s32[256]{0:T(256)S(1)}, s32[256]{0:T(256)}, u32[]{:S(2)}) copy-start(s32[256]{0:T(256)} %param.15) | copy-start | bytes 3076
  353.6 25.7 %copy-start.4 = (f32[64]{0:T(128)}, f32[64]{0:T(128)S(1)}, u32[]{:S(2)}) copy-start(f32[64]{0:T(128)S(1)} %psum.21) | copy-start | bytes 772
Sparse Core Ops, SparseCore 0:
  214.1 65.5 reduce-scatter.1
where the time goes:
time: 391 us; the launch traced here: 386 us
  local copies, waits for them, and re-layouts  107 us (27%)
  blocking collectives  95.1 us (24%)
  matrix products  87.2 us (22%)
  waiting for transfers between devices  64.8 us (17%)
  between operations  14.3 us (4%)
  other arithmetic  12.4 us (3%)
  loops' own time  5.64 us (1%)
    gather x8, local copies, waits for them, and re-layouts, one_block(): picked = jnp.take(rows, factor_of_bus, axis=1)  101 us
    dot_general x8, matrix products, one_block(): lax.dot_general(injections, ptdf, (((1,), (1,)), ((), ())), preferred_ele...  77.1 us
    psum x1, blocking collectives, per_device(): overload = lax.psum(share, 'line')  72.9 us
    reduce_scatter x1, waiting for transfers between devices, per_device(): lax.psum_scatter(pieces.reshape(block_rows * lax.axis_size('bus'), ptdf.s...  64.8 us
    psum x1, blocking collectives, per_device(): moved, total = lax.psum((moved_part, jnp.sum(emphasis)), 'bus')  22.2 us
    dot_general x1, matrix products, per_device(): lax.dot_general(normals(directions, shifts, 0, scenarios) + proposal_mean...  9.05 us
  transfers between devices with their start and end apart: 1, of which 1 were waited for; matrix products, arithmetic and copies ran while one was open for 0% of the time, Pallas kernels for 0%

commit v1 on v0

v1 whole, which is shorter than its diff:
```python
import functools
import math

import jax
import jax.numpy as jnp
from jax import lax
from jax.experimental import pallas as pl
from jax.experimental.pallas import tpu as pltpu
from jax.sharding import PartitionSpec as P

MESH = pl.DeviceIdType.MESH
POINTS = 128
SHARP = 8.0
F32 = jnp.float32
BF16 = jnp.bfloat16
NT = (((1,), (1,)), ((), ()))
NN = (((1,), (0,)), ((), ()))
PIECES = 2

CENTRAL = (
    2.81022636e-08,
    3.43273939e-07,
    -3.5233877e-06,
    -4.39150654e-06,
    0.00021858087,
    -0.00125372503,
    -0.00417768164,
    0.246640727,
    1.50140941,
)
TAIL = (
    -0.000200214257,
    0.000100950558,
    0.00134934322,
    -0.00367342844,
    0.00573950773,
    -0.0076224613,
    0.00943887047,
    1.00167406,
    2.83297682,
)


def dot(a, b, dims):
    return lax.dot_general(a, b, dims, preferred_element_type=F32)


def split(x):
    hi = x.astype(BF16)
    return hi, (x - hi.astype(F32)).astype(BF16)


def draw(digits):
    x = (2 * lax.shift_right_arithmetic(digits, 7) + 1).astype(F32) * (1.0 / 8388608.0) - 1.0
    w = -jnp.log((1.0 - x) * (1.0 + x))
    near = w < 5.0
    t = jnp.where(near, w - 2.5, jnp.sqrt(w) - 3.0)
    p = jnp.where(near, CENTRAL[0], TAIL[0])
    for a, b in zip(CENTRAL[1:], TAIL[1:]):
        p = jnp.where(near, a, b) + p * t
    return math.sqrt(2.0) * x * p


def kernel(
    nz,
    nl,
    ptdf_h,
    base_h,
    gain_h,
    fob_h,
    rating_h,
    dirs_h,
    shifts_h,
    chol_h,
    mean_h,
    flows_o,
    overload_o,
    weight_o,
    newmean_o,
    ptdf,
    base,
    gain,
    fob,
    rating,
    dirs,
    shifts,
    chol,
    mean,
    m_all,
    ring_p,
    ring_m,
    table,
    n_hi,
    n_lo,
    c_hi,
    c_lo,
    lik,
    base_row,
    base_in,
    send,
    recv,
    share,
    plane_in,
    plane_sum,
    deep_in,
    over,
    load_sem,
    ps,
    pr,
    ms,
    mr,
    bs,
    br,
    fs,
    fr,
    ls,
    lr,
    ds,
    dr,
):
    z = lax.axis_index("bus")
    me = lax.axis_index("line")
    lines, buses = ptdf.shape
    factors = chol.shape[0]
    half = nz // 2
    blocks = [(k, min(1024, buses - k)) for k in range(0, buses, 1024)]

    small = [
        (fob_h, fob),
        (gain_h, gain),
        (base_h, base),
        (rating_h, rating),
        (dirs_h, dirs),
        (shifts_h, shifts),
        (chol_h, chol),
        (mean_h, mean),
    ]
    loads = [pltpu.make_async_copy(a, b, load_sem.at[i]) for i, (a, b) in enumerate(small)]
    for i, (k, size) in enumerate(blocks):
        loads.append(
            pltpu.make_async_copy(
                ptdf_h.at[:, pl.ds(k, size)], ptdf.at[:, pl.ds(k, size)], load_sem.at[len(small) + i]
            )
        )
    for copy in loads:
        copy.start()

    barrier = pltpu.get_barrier_semaphore()

    def greet_z(d, carry):
        pl.semaphore_signal(
            barrier, inc=1, device_id={"bus": lax.rem(z + d, nz)}, device_id_type=MESH
        )
        return carry

    def greet_l(d, carry):
        pl.semaphore_signal(
            barrier, inc=1, device_id={"line": lax.rem(me + d, nl)}, device_id_type=MESH
        )
        return carry

    lax.fori_loop(1, nz, greet_z, 0)
    lax.fori_loop(1, nl, greet_l, 0)

    for copy in loads[: len(small)]:
        copy.wait()
    acc = jnp.zeros((lines, factors), F32)
    for i, (k, size) in enumerate(blocks):
        loads[len(small) + i].wait()
        rows = ptdf[:, pl.ds(k, size)]
        g_hi, g_lo = split(gain[:, pl.ds(k, size)])
        which = fob[:, pl.ds(k, size)]
        hit = lax.broadcasted_iota(jnp.int32, (factors, size), 0) == which
        acc += dot(rows, jnp.where(hit, g_hi.astype(F32), 0.0).astype(BF16), NT)
        acc += dot(rows, jnp.where(hit, g_lo.astype(F32), 0.0).astype(BF16), NT)
    m_all[...] = acc.reshape(m_all.shape)

    pl.semaphore_wait(barrier, nz + nl - 2)

    wide = factors // PIECES
    right = lax.rem(z + 1, nz)
    left = lax.rem(z + nz - 1, nz)

    def lanes(piece):
        return pl.ds(piece * wide, wide)

    def hop(source, ring, t, piece, send_sem, recv_sem, target):
        return pltpu.make_async_remote_copy(
            src_ref=source,
            dst_ref=ring.at[t, :, lanes(piece)],
            send_sem=send_sem.at[t, piece],
            recv_sem=recv_sem.at[t, piece],
            device_id={"bus": target},
            device_id_type=MESH,
        )

    def shadow(t):
        if t == 0:
            point = lax.broadcasted_iota(jnp.int32, (POINTS, factors), 0)
            digits = jnp.zeros((POINTS, factors), jnp.int32)
            for bit in range(7):
                picked = lax.shift_right_logical(point, bit) & 1
                digits = digits ^ (picked * dirs[bit : bit + 1, :])
            table[...] = digits
            hi, lo = split(chol[...])
            c_hi[...] = hi
            c_lo[...] = lo
        if t == 1:
            row = jnp.zeros((16, lines), F32)
            for k, size in blocks:
                hi, lo = split(base[:, pl.ds(k, size)])
                both = jnp.concatenate([hi.astype(F32), lo.astype(F32), jnp.zeros((14, size), F32)], axis=0)
                row += dot(both.astype(BF16), ptdf[:, pl.ds(k, size)], NT)
            total_row = row[0:1, :] + row[1:2, :]
            base_row[0:1, :] = total_row[:, 0 : lines // 2]
            base_row[1:2, :] = total_row[:, lines // 2 :]
        rows = pl.ds(t * POINTS, POINTS)
        normal = draw(table[...] ^ shifts[t : t + 1, :])
        hi, lo = split(normal)
        n_hi[rows, :] = hi
        n_lo[rows, :] = lo
        m_hi, m_lo = split(mean[...])
        both = jnp.concatenate(
            [m_hi.astype(F32), m_lo.astype(F32), jnp.zeros((14, factors), F32)], axis=0
        ).astype(BF16)
        first = dot(both, hi, NT)
        second = dot(both, lo, NT)
        lik[t : t + 1, :] = jnp.exp(-(first[0:1, :] + (first[1:2, :] + second[0:1, :])))

    sent = []
    for t in range(half):
        for piece in range(PIECES):
            if t == 0:
                source = m_all.at[lax.rem(z + half, nz), :, lanes(piece)]
            else:
                sent_in = hop(ring_p.at[t - 1, :, lanes(piece)], ring_p, t - 1, piece, ps, pr, right)
                sent_in.wait_recv()
                ring_p[t - 1, :, lanes(piece)] += m_all[lax.rem(z + half - t, nz), :, lanes(piece)]
                source = ring_p.at[t - 1, :, lanes(piece)]
            copy = hop(source, ring_p, t, piece, ps, pr, right)
            copy.start()
            sent.append(copy)
            if t == half - 1:
                continue
            if t == 0:
                source = m_all.at[lax.rem(z + nz - half + 1, nz), :, lanes(piece)]
            else:
                sent_in = hop(ring_m.at[t - 1, :, lanes(piece)], ring_m, t - 1, piece, ms, mr, left)
                sent_in.wait_recv()
                ring_m[t - 1, :, lanes(piece)] += m_all[
                    lax.rem(z + nz - half + 1 + t, nz), :, lanes(piece)
                ]
                source = ring_m.at[t - 1, :, lanes(piece)]
            copy = hop(source, ring_m, t, piece, ms, mr, left)
            copy.start()
            sent.append(copy)
        shadow(t)
        if t == 1:
            for d in range(1, nz):
                peer = lax.rem(z + d, nz)
                copy = pltpu.make_async_remote_copy(
                    src_ref=base_row,
                    dst_ref=base_in.at[z],
                    send_sem=bs.at[d],
                    recv_sem=br.at[z],
                    device_id={"bus": peer},
                    device_id_type=MESH,
                )
                copy.start()
                sent.append(copy)
            base_in[z] = base_row[...]

    for d in range(1, nz):
        peer = lax.rem(z + d, nz)
        pltpu.make_async_remote_copy(
            src_ref=base_row,
            dst_ref=base_in.at[peer],
            send_sem=bs.at[d],
            recv_sem=br.at[peer],
            device_id={"bus": peer},
            device_id_type=MESH,
        ).wait_recv()
    own_lines = lines // nz
    base_sum = base_in[0]
    for j in range(1, nz):
        base_sum = base_sum + base_in[j]
    base_line = jnp.concatenate([base_sum[0:1, :], base_sum[1:2, :]], axis=1)
    mine = lax.broadcasted_iota(jnp.int32, (own_lines, lines), 1) == (
        lax.broadcasted_iota(jnp.int32, (own_lines, lines), 0) + z * own_lines
    )
    base_col = jnp.sum(jnp.where(mine, base_line, 0.0), axis=1, keepdims=True)
    rate_col = jnp.sum(jnp.where(mine, rating[...].astype(F32) * 0.01, 0.0), axis=1, keepdims=True)
    steep = SHARP / rate_col

    total_m = m_all[z]
    parts = []
    for piece in range(PIECES):
        hop(ring_p.at[half - 1, :, lanes(piece)], ring_p, half - 1, piece, ps, pr, right).wait_recv()
        hop(ring_m.at[half - 2, :, lanes(piece)], ring_m, half - 2, piece, ms, mr, left).wait_recv()
    total_m = total_m + ring_p[half - 1] + ring_m[half - 2]

    h, l = split(total_m)
    g = dot(h, c_hi[...], NN) + (dot(l, c_hi[...], NN) + dot(h, c_lo[...], NN))
    const = jnp.sum(g * mean[...], axis=1, keepdims=True) + base_col
    gh, gl = split(g)
    both = jnp.concatenate([gh.astype(F32), gl.astype(F32)], axis=0).astype(BF16)
    low_lane = lax.broadcasted_iota(jnp.int32, (8, POINTS), 1) < POINTS // 2
    for k in range(8):
        rows = pl.ds(k * POINTS, POINTS)
        first = dot(both, n_hi[rows, :], NT)
        second = dot(gh, n_lo[rows, :], NT)
        x = first[0:own_lines, :] + (first[own_lines:, :] + second) + const
        v = jnp.abs(x) * steep - SHARP
        soft = jnp.maximum(v, 0.0) + jnp.log1p(jnp.exp(-jnp.abs(v)))
        share[k : k + 1, :] = jnp.sum(soft, axis=0, keepdims=True) * (1.0 / (SHARP * lines * nl))
        top, low = x[0:8, :], x[8:16, :]
        send[2 * k] = jnp.where(low_lane, top, pltpu.roll(low, POINTS // 2, 1))
        send[2 * k + 1] = jnp.where(low_lane, pltpu.roll(top, POINTS // 2, 1), low)

    def plane_copy(peer, slot, d):
        return pltpu.make_async_remote_copy(
            src_ref=share,
            dst_ref=plane_in.at[slot],
            send_sem=ls.at[d],
            recv_sem=lr.at[slot],
            device_id={"line": peer},
            device_id_type=MESH,
        )

    def plane_start(d, carry):
        plane_copy(lax.rem(me + d, nl), me, d).start()
        return carry

    def plane_wait(d, carry):
        peer = lax.rem(me + d, nl)
        plane_copy(peer, peer, d).wait()
        return carry

    def flow_copy(peer, slot, d):
        return pltpu.make_async_remote_copy(
            src_ref=send.at[peer],
            dst_ref=recv.at[slot],
            send_sem=fs.at[d],
            recv_sem=fr.at[slot],
            device_id={"bus": peer},
            device_id_type=MESH,
        )

    def flow_start(d, carry):
        flow_copy(lax.rem(z + d, nz), z, d).start()
        return carry

    def flow_wait(d, carry):
        peer = lax.rem(z + d, nz)
        flow_copy(peer, peer, d).wait()
        return carry

    def deep_copy(peer, slot, d):
        return pltpu.make_async_remote_copy(
            src_ref=plane_sum,
            dst_ref=deep_in.at[slot],
            send_sem=ds.at[d],
            recv_sem=dr.at[slot],
            device_id={"bus": peer},
            device_id_type=MESH,
        )

    def deep_start(d, carry):
        deep_copy(lax.rem(z + d, nz), z, d).start()
        return carry

    def deep_wait(d, carry):
        peer = lax.rem(z + d, nz)
        deep_copy(peer, peer, d).wait()
        return carry

    lax.fori_loop(1, nl, plane_start, 0)
    lax.fori_loop(1, nz, flow_start, 0)
    plane_in[me] = share[...]
    recv[z] = send[z]
    lax.fori_loop(1, nl, plane_wait, 0)
    partial = plane_in[0]
    for j in range(1, nl):
        partial = partial + plane_in[j]
    plane_sum[...] = partial
    lax.fori_loop(1, nz, deep_start, 0)
    deep_in[z] = partial

    lax.fori_loop(1, nz, flow_wait, 0)
    tiles = []
    for j in range(nz):
        tile = recv[j]
        tiles.append(tile)
        tiles.append(pltpu.roll(tile, POINTS // 2, 1))
    by_line = jnp.concatenate(tiles, axis=0)
    flows_o[...] = jnp.transpose(by_line)[0 : POINTS // 2, :]

    lax.fori_loop(1, nz, deep_wait, 0)
    total_over = deep_in[0]
    for j in range(1, nz):
        total_over = total_over + deep_in[j]
    over[...] = total_over
    emphasis = lik[...] * total_over
    total = jnp.sum(jnp.sum(emphasis, axis=1, keepdims=True), axis=0, keepdims=True)
    inverse = 1.0 / total
    flat = jnp.concatenate([emphasis[k : k + 1, :] for k in range(8)], axis=1)
    e_hi, e_lo = split(flat)
    both = jnp.concatenate(
        [e_hi.astype(F32), e_lo.astype(F32), jnp.zeros((14, flat.shape[1]), F32)], axis=0
    ).astype(BF16)
    first = dot(both, n_hi[...], NN)
    second = dot(both, n_lo[...], NN)
    moved = first[0:1, :] + (first[1:2, :] + second[0:1, :])
    newmean_o[...] = mean[...] + moved * inverse
    row = over[pl.ds(z // 2, 1), :]
    like_row = lik[pl.ds(z // 2, 1), :]
    odd = lax.rem(z, 2) == 1
    row = jnp.where(odd, row[:, POINTS // 2 :], row[:, 0 : POINTS // 2])
    like_row = jnp.where(odd, like_row[:, POINTS // 2 :], like_row[:, 0 : POINTS // 2])
    overload_o[...] = row
    weight_o[...] = (float(8 * POINTS) * like_row) * row * inverse

    for copy in sent:
        copy.wait_send()


def per_device(nz, nl, ptdf, base, gain, fob, rating, dirs, shifts, chol, mean):
    lines, buses = ptdf.shape
    factors = chol.shape[0]
    half = nz // 2
    own = lines // nz
    scen = shifts.shape[0] * POINTS
    vm, dma = pltpu.VMEM, pltpu.SemaphoreType.DMA
    anywhere = pl.BlockSpec(memory_space=pl.ANY)
    inside = pl.BlockSpec(memory_space=pltpu.VMEM)
    n_loads = 8 + -(-buses // 1024)
    flows, overload, weight, new_mean = pl.pallas_call(
        functools.partial(kernel, nz, nl),
        out_shape=(
            jax.ShapeDtypeStruct((scen // nz, lines), F32),
            jax.ShapeDtypeStruct((1, scen // nz), F32),
            jax.ShapeDtypeStruct((1, scen // nz), F32),
            jax.ShapeDtypeStruct((1, factors), F32),
        ),
        in_specs=[anywhere] * 9,
        out_specs=(inside,) * 4,
        scratch_shapes=[
            vm((lines, buses), BF16),
            vm((1, buses), F32),
            vm((1, buses), F32),
            vm((1, buses), jnp.int32),
            vm((1, lines), jnp.int32),
            vm(dirs.shape, jnp.int32),
            vm(shifts.shape, jnp.int32),
            vm(chol.shape, F32),
            vm((1, factors), F32),
            vm((nz, own, factors), F32),
            vm((half, own, factors), F32),
            vm((half - 1, own, factors), F32),
            vm((POINTS, factors), jnp.int32),
            vm((scen, factors), BF16),
            vm((scen, factors), BF16),
            vm(chol.shape, BF16),
            vm(chol.shape, BF16),
            vm((8, POINTS), F32),
            vm((2, POINTS), F32),
            vm((nz, 2, POINTS), F32),
            vm((nz, 8, POINTS), F32),
            vm((nz, 8, POINTS), F32),
            vm((8, POINTS), F32),
            vm((nl, 8, POINTS), F32),
            vm((8, POINTS), F32),
            vm((nz, 8, POINTS), F32),
            vm((8, POINTS), F32),
            dma((n_loads,)),
            dma((half, PIECES)),
            dma((half, PIECES)),
            dma((half - 1, PIECES)),
            dma((half - 1, PIECES)),
            dma((nz,)),
            dma((nz,)),
            dma((nz,)),
            dma((nz,)),
            dma((nl,)),
            dma((nl,)),
            dma((nz,)),
            dma((nz,)),
        ],
        compiler_params=pltpu.CompilerParams(
            collective_id=0, has_side_effects=True, vmem_limit_bytes=40 * 1024 * 1024
        ),
    )(
        ptdf,
        base.reshape(1, buses),
        gain.reshape(1, buses),
        fob.reshape(1, buses),
        rating.reshape(1, lines),
        dirs,
        shifts,
        chol,
        mean.reshape(1, factors),
    )
    return flows, overload.reshape(-1), weight.reshape(-1), new_mean.reshape(-1)


def solution(mesh):
    nz, nl = mesh.shape["bus"], mesh.shape["line"]
    return jax.shard_map(
        functools.partial(per_device, nz, nl),
        mesh=mesh,
        in_specs=(P("line", "bus"), P("bus"), P("bus"), P("bus"), P("line"), P(), P(), P(), P()),
        out_specs=(P("bus", "line"), P("bus"), P("bus"), P()),
        check_vma=False,
    )
```

time: 391 us -> 70.6 us (0.18); the launches traced: 386 us -> 70 us
  local copies, waits for them, and re-layouts: 107 us -> 10.6 us
  blocking collectives: 95.1 us -> 0 us
  matrix products: 87.2 us -> 0 us
  waiting for transfers between devices: 64.8 us -> 0 us
  Pallas kernels: 0 us -> 58.8 us
  between operations: 14.3 us -> 0.66 us
  other arithmetic: 12.4 us -> 0 us
  loops' own time: 5.64 us -> 0 us
    gather x8 -> x0, local copies, waits for them, and re-layouts: 101 us -> none  [one_block(): picked = jnp.take(rows, factor_of_bus, axis=1)]
    psum x2 -> x0, blocking collectives: 95.1 us -> none  [the longest x1 72.9 us: per_device(): overload = lax.psum(share, 'line')]
    dot_general x11 -> x0, matrix products: 87.2 us -> none  [the longest x8 77.1 us: one_block(): lax.dot_general(injections, ptdf, (((1,), (1,)), ((), ())), preferred_ele...]
    reduce_scatter x1 -> x0, waiting for transfers between devices: 64.8 us -> none  [per_device(): lax.psum_scatter(pieces.reshape(block_rows * lax.axis_size('bus'), ptdf.s...]
    pallas_call x0 -> x1, Pallas kernels: none -> 58.8 us  [per_device(): pl.pallas_call(functools.partial(kernel, nz, nl), out_shape=(jax.ShapeDty...]
    reduce_sum x3 -> x0, other arithmetic: 8.35 us -> none  [the longest x2 7.36 us: normals(): offset = jnp.sum(chosen[:, :, None] * shifts[None, :, :], axis=1)]
    unnamed x14 -> x16, local copies, waits for them, and re-layouts: 0.04 us -> 8.28 us
    another operation x1 -> x0, loops' own time: 5.64 us -> none  [per_device(): lax.map(one_block, jnp.arange(block_rows * lax.axis_size('bus') // block_...]
  transfers between devices with their start and end apart: 1 -> 0, of which waited for: 1 -> 0; matrix products, arithmetic and copies ran while one was open for 0% -> 0% of each run, Pallas kernels for 0% -> 0%
where the time goes in v1:
time: 70.6 us; the launch traced here: 70 us
  Pallas kernels  58.8 us (83%)
  local copies, waits for them, and re-layouts  10.6 us (15%)
    pallas_call x1, Pallas kernels, per_device(): pl.pallas_call(functools.partial(kernel, nz, nl), out_shape=(jax.ShapeDty...  58.8 us
    unnamed x16, local copies, waits for them, and re-layouts  8.28 us

profile of v1, /device:TPU:1, one launch (start us, length us, event | category | flops | bytes accessed | tf_op | source)
XLA Modules:
  0.0 70.0 jit_solution(1390806016246099225)
XLA Ops:
  0.6 0.8 %reshape.32.base_h = f32[1,6272]{1,0:T(1,128)S(1)} reshape(f32[6272]{0:T(1024)} %param.10) | data formatting | bytes 50176 | tf_op jit(solution)/shard_map/reshape | solution.py:494
  1.4 0.8 %reshape.33.gain_h = f32[1,6272]{1,0:T(1,128)S(1)} reshape(f32[6272]{0:T(1024)} %param.11) | data formatting | bytes 50176 | tf_op jit(solution)/shard_map/reshape | solution.py:495
  2.2 0.8 %reshape.34.fob_h = s32[1,6272]{1,0:T(1,128)S(1)} reshape(s32[6272]{0:T(1024)} %param.12) | data formatting | bytes 50176 | tf_op jit(solution)/shard_map/reshape | solution.py:496
  2.9 0.0 copy-start
  3.0 1.9 %copy-done = bf16[256,6272]{1,0:T(8,128)(2,1)S(1)} copy-done((bf16[256,6272]{1,0:T(8,128)(2,1)S(1)}, bf16[256,6272]{1,0:T(8,128)(2,1)}, u32[]{:S(2)}) %copy-start) | copy-done | bytes 3211288
  4.9 0.0 copy-start.1
  4.9 1.2 %copy-done.1 = f32[512,512]{1,0:T(8,128)S(1)} copy-done((f32[512,512]{1,0:T(8,128)S(1)}, f32[512,512]{1,0:T(8,128)}, u32[]{:S(2)}) %copy-start.1) | copy-done | bytes 1048600
  6.1 0.0 copy-start.2
  6.1 0.8 %copy-done.2 = s32[30,512]{1,0:T(8,128)S(1)} copy-done((s32[30,512]{1,0:T(8,128)S(1)}, s32[30,512]{1,0:T(8,128)}, u32[]{:S(2)}) %copy-start.2) | copy-done | bytes 61464
  6.9 0.0 copy-start.3
  6.9 0.7 %copy-done.3 = s32[8,512]{1,0:T(8,128)S(1)} copy-done((s32[8,512]{1,0:T(8,128)S(1)}, s32[8,512]{1,0:T(8,128)}, u32[]{:S(2)}) %copy-start.3) | copy-done | bytes 16408
  7.6 0.0 copy-start.4
  7.6 0.7 copy-done.4
  8.3 0.0 copy-start.5
  8.3 0.7 copy-done.5
  9.0 58.8 %shard_map.120 = (f32[64,256]{1,0:T(8,128)S(1)}, f32[1,64]{1,0:T(1,128)S(1)}, f32[1,64]{1,0:T(1,128)S(1)}, f32[1,512]{1,0:T(1,128)S(1)}) custom-call(bf16[256,6272]{1,0:T(8,128)(2,1)S(1)} %copy-done, f32[1,6272]{1,0:T(1,128)S(1)} %reshape.32.base_h, f32[1,6272]{1,0:T(1,128)S(1)} %reshape.33.gain_h, s32[1,6272]{1,0:T(1,128)S(1)} %reshape.34.fob_h, ...), custom_call_target="tpu_custom_call" | custom-call | tf_op jit(solution)/shard_map/pallas_call | solution.py:437
  67.8 0.6 copy.17
  68.4 0.5 copy.18
  68.9 0.5 copy.19
  69.4 0.6 copy.20
Async XLA Ops:
  2.9 1.9 %copy-start = (bf16[256,6272]{1,0:T(8,128)(2,1)S(1)}, bf16[256,6272]{1,0:T(8,128)(2,1)}, u32[]{:S(2)}) copy-start(bf16[256,6272]{1,0:T(8,128)(2,1)} %ptdf_h.1) | copy-start | bytes 9633796
  4.9 1.2 %copy-start.1 = (f32[512,512]{1,0:T(8,128)S(1)}, f32[512,512]{1,0:T(8,128)}, u32[]{:S(2)}) copy-start(f32[512,512]{1,0:T(8,128)} %chol_h.1) | copy-start | bytes 3145732
  6.1 0.8 %copy-start.2 = (s32[30,512]{1,0:T(8,128)S(1)}, s32[30,512]{1,0:T(8,128)}, u32[]{:S(2)}) copy-start(s32[30,512]{1,0:T(8,128)} %dirs_h.1) | copy-start | bytes 184324
  6.9 0.7 %copy-start.3 = (s32[8,512]{1,0:T(8,128)S(1)}, s32[8,512]{1,0:T(8,128)}, u32[]{:S(2)}) copy-start(s32[8,512]{1,0:T(8,128)} %shifts_h.1) | copy-start | bytes 49156
  7.6 0.7 copy-start.4
  8.3 0.7 copy-start.5

commit v2 on v1

v2 whole, which is shorter than its diff:
```python
import functools
import math

import jax
import jax.numpy as jnp
from jax import lax
from jax.experimental import pallas as pl
from jax.experimental.pallas import tpu as pltpu
from jax.sharding import PartitionSpec as P

MESH = pl.DeviceIdType.MESH
POINTS = 128
SHARP = 8.0
F32 = jnp.float32
BF16 = jnp.bfloat16
NT = (((1,), (1,)), ((), ()))
NN = (((1,), (0,)), ((), ()))
PIECES = 2
PLUS = (6, 3, 0)
MINUS = (5, 2, 0)
GAPS = ((0, 1, 2), (3, 4, 5), (6, 7))

CENTRAL = (
    2.81022636e-08,
    3.43273939e-07,
    -3.5233877e-06,
    -4.39150654e-06,
    0.00021858087,
    -0.00125372503,
    -0.00417768164,
    0.246640727,
    1.50140941,
)
TAIL = (
    -0.000200214257,
    0.000100950558,
    0.00134934322,
    -0.00367342844,
    0.00573950773,
    -0.0076224613,
    0.00943887047,
    1.00167406,
    2.83297682,
)


def dot(a, b, dims):
    return lax.dot_general(a, b, dims, preferred_element_type=F32)


def split(x):
    hi = x.astype(BF16)
    return hi, (x - hi.astype(F32)).astype(BF16)


def draw(digits):
    x = (2 * lax.shift_right_arithmetic(digits, 7) + 1).astype(F32) * (1.0 / 8388608.0) - 1.0
    w = -jnp.log((1.0 - x) * (1.0 + x))
    near = w < 5.0
    t = jnp.where(near, w - 2.5, jnp.sqrt(w) - 3.0)
    p = jnp.where(near, CENTRAL[0], TAIL[0])
    for a, b in zip(CENTRAL[1:], TAIL[1:]):
        p = jnp.where(near, a, b) + p * t
    return math.sqrt(2.0) * x * p


def next_stop(stops, k):
    return max(c for c in stops if c < k)


def far_first(offsets, sizes):
    reach = [sum(min(o, n - o) for o, n in zip(off, sizes)) for off in offsets]
    return [offsets[i] for i in sorted(range(len(offsets)), key=lambda i: -reach[i])]


def kernel(
    nz,
    nl,
    ptdf_h,
    base_h,
    gain_h,
    fob_h,
    rating_h,
    dirs_h,
    shifts_h,
    chol_h,
    mean_h,
    flows_o,
    overload_o,
    weight_o,
    newmean_o,
    ptdf,
    base,
    gain,
    fob,
    rating,
    dirs,
    shifts,
    chol,
    mean,
    m_all,
    ring_p,
    ring_m,
    table,
    n_hi,
    n_lo,
    c_hi,
    c_lo,
    lik,
    base_row,
    base_in,
    send,
    recv,
    share,
    pair_in,
    chip_sum,
    plane_in,
    plane_sum,
    deep_in,
    over,
    load_sem,
    ps,
    pr,
    ms,
    mr,
    bs,
    br,
    fs,
    fr,
    cs,
    cr,
    ls,
    lr,
    ds,
    dr,
):
    z = lax.axis_index("bus")
    me = lax.axis_index("line")
    lines, buses = ptdf.shape
    factors = chol.shape[0]
    half = nz // 2
    cut = buses // 2 // 128 * 128 + 128
    blocks = [(0, cut), (cut, buses - cut)]
    chip, core = me // 2, lax.rem(me, 2)
    row_of, col_of = chip // 4, lax.rem(chip, 4)
    z_order = [d for (d,) in far_first([(d,) for d in range(1, nz)], (nz,))]
    plane_order = far_first([(i, j) for i in range(4) for j in range(4) if i + j > 0], (4, 4))

    def chip_at(i, j):
        return lax.rem(row_of + i, 4) * 4 + lax.rem(col_of + j, 4)

    first = [(fob_h, fob), (gain_h, gain), (base_h, base)]
    later = [
        (rating_h, rating),
        (dirs_h, dirs),
        (shifts_h, shifts),
        (chol_h, chol),
        (mean_h, mean),
    ]
    pairs = list(first)
    for k, size in blocks:
        pairs.append((ptdf_h.at[:, pl.ds(k, size)], ptdf.at[:, pl.ds(k, size)]))
    pairs += later
    loads = [pltpu.make_async_copy(a, b, load_sem.at[i]) for i, (a, b) in enumerate(pairs)]
    for copy in loads:
        copy.start()

    barrier = pltpu.get_barrier_semaphore()

    def greet_z(d, carry):
        pl.semaphore_signal(
            barrier, inc=1, device_id={"bus": lax.rem(z + d, nz)}, device_id_type=MESH
        )
        return carry

    lax.fori_loop(1, nz, greet_z, 0)
    for i, j in plane_order:
        pl.semaphore_signal(
            barrier,
            inc=1,
            device_id={"line": chip_at(i, j) * 2 + core},
            device_id_type=MESH,
        )
    pl.semaphore_signal(
        barrier, inc=1, device_id={"line": chip * 2 + 1 - core}, device_id_type=MESH
    )

    wide = factors // PIECES

    factor = lax.broadcasted_iota(jnp.int32, (wide, 128), 0).astype(F32).astype(BF16)
    nothing = jnp.zeros((wide, 128), BF16)

    def gather(piece):
        acc = None
        for i, (k, size) in enumerate(blocks):
            if piece == 0:
                loads[len(first) + i].wait()
            g_hi, g_lo = split(gain[pl.ds(k, size)].reshape(1, size))
            which = (fob[pl.ds(k, size)].reshape(1, size) - wide * piece).astype(F32).astype(BF16)
            hi, lo = [], []
            for j in range(0, size, 128):
                hit = factor == jnp.broadcast_to(which[:, j : j + 128], (wide, 128))
                hi.append(jnp.where(hit, jnp.broadcast_to(g_hi[:, j : j + 128], (wide, 128)), nothing))
                lo.append(jnp.where(hit, jnp.broadcast_to(g_lo[:, j : j + 128], (wide, 128)), nothing))
            stack = [jnp.concatenate(hi, axis=1), jnp.concatenate(lo, axis=1)]
            if piece == 0:
                b_hi, b_lo = split(base[pl.ds(k, size)].reshape(1, size))
                stack.append(
                    jnp.concatenate(
                        [b_hi.astype(F32), b_lo.astype(F32), jnp.zeros((14, size), F32)], axis=0
                    ).astype(BF16)
                )
            part = dot(jnp.concatenate(stack, axis=0), ptdf[:, pl.ds(k, size)], NT)
            acc = part if acc is None else acc + part
        by_line = jnp.transpose(acc[0:wide] + acc[wide : 2 * wide])
        m_all[:, :, wide * piece : wide * (piece + 1)] = by_line.reshape(nz, lines // nz, wide)
        if piece == 0:
            total_row = acc[2 * wide : 2 * wide + 1] + acc[2 * wide + 1 : 2 * wide + 2]
            base_row[0:1, :] = total_row[:, 0 : lines // 2]
            base_row[1:2, :] = total_row[:, lines // 2 :]

    def lanes(piece):
        return pl.ds(piece * wide, wide)

    sides = (
        (1, PLUS, half, ring_p, ps, pr),
        (-1, MINUS, half - 1, ring_m, ms, mr),
    )

    def toward(sign, k):
        return lax.rem(z + sign * k + nz, nz)

    def hop(side, k, piece, source):
        sign, stops, far, ring, send_sem, recv_sem = side
        return pltpu.make_async_remote_copy(
            src_ref=source,
            dst_ref=ring.at[k, :, lanes(piece)],
            send_sem=send_sem.at[k, piece],
            recv_sem=recv_sem.at[k, piece],
            device_id={"bus": toward(sign, k - next_stop(stops, k))},
            device_id_type=MESH,
        )

    def arrived(side, k, piece):
        hop(side, k, piece, side[3].at[k, :, lanes(piece)]).wait_recv()

    sent = []

    def direct(piece):
        far = max(side[2] for side in sides)
        for k in range(far, 0, -1):
            for side in sides:
                if k <= side[2] and k not in side[1]:
                    copy = hop(side, k, piece, m_all.at[toward(side[0], k), :, lanes(piece)])
                    copy.start()
                    sent.append(copy)

    def merge(level, piece):
        for side in sides:
            sign, stops, far, ring, _, _ = side
            if level >= len(stops) - 1:
                continue
            c = stops[level]
            members = [k for k in range(far, 0, -1) if next_stop(stops, k) == c]
            block = m_all[toward(sign, c), :, lanes(piece)]
            for k in members:
                arrived(side, k, piece)
                block = block + ring[k, :, lanes(piece)]
            ring[members[0], :, lanes(piece)] = block
            copy = hop(side, c, piece, ring.at[members[0], :, lanes(piece)])
            copy.start()
            sent.append(copy)

    def prepare():
        for copy in loads[len(first) + len(blocks) :]:
            copy.wait()
        point = lax.broadcasted_iota(jnp.int32, (POINTS, factors), 0)
        digits = jnp.zeros((POINTS, factors), jnp.int32)
        for bit in range(7):
            picked = lax.shift_right_logical(point, bit) & 1
            digits = digits ^ (picked * dirs[bit : bit + 1, :])
        table[...] = digits
        hi, lo = split(chol[...])
        c_hi[...] = hi
        c_lo[...] = lo

    def shadow(t):
        rows = pl.ds(t * POINTS, POINTS)
        normal = draw(table[...] ^ shifts[t : t + 1, :])
        hi, lo = split(normal)
        n_hi[rows, :] = hi
        n_lo[rows, :] = lo
        m_hi, m_lo = split(mean[...].reshape(1, factors))
        both = jnp.concatenate(
            [m_hi.astype(F32), m_lo.astype(F32), jnp.zeros((14, factors), F32)], axis=0
        ).astype(BF16)
        first = dot(both, hi, NT)
        second = dot(both, lo, NT)
        lik[t : t + 1, :] = jnp.exp(-(first[0:1, :] + (first[1:2, :] + second[0:1, :])))

    def base_copy(d, slot):
        return pltpu.make_async_remote_copy(
            src_ref=base_row,
            dst_ref=base_in.at[slot],
            send_sem=bs.at[d],
            recv_sem=br.at[slot],
            device_id={"bus": lax.rem(z + d, nz)},
            device_id_type=MESH,
        )

    for copy in loads[: len(first)]:
        copy.wait()
    gather(0)
    pl.semaphore_wait(barrier, nz + nl // 2 - 1)
    direct(0)
    for d in z_order:
        copy = base_copy(d, z)
        copy.start()
        sent.append(copy)
    base_in[z] = base_row[...]
    for piece in range(1, PIECES):
        gather(piece)
        direct(piece)
    prepare()
    for level in range(len(PLUS)):
        for t in GAPS[level]:
            shadow(t)
        if level < len(PLUS) - 1:
            for piece in range(PIECES):
                merge(level, piece)

    for d in z_order:
        base_copy(d, lax.rem(z + d, nz)).wait_recv()
    own_lines = lines // nz
    base_sum = base_in[0]
    for j in range(1, nz):
        base_sum = base_sum + base_in[j]
    base_line = jnp.concatenate([base_sum[0:1, :], base_sum[1:2, :]], axis=1)
    mine = lax.broadcasted_iota(jnp.int32, (own_lines, lines), 1) == (
        lax.broadcasted_iota(jnp.int32, (own_lines, lines), 0) + z * own_lines
    )
    base_col = jnp.sum(jnp.where(mine, base_line, 0.0), axis=1, keepdims=True)
    rate_col = jnp.sum(jnp.where(mine, rating[...].reshape(1, lines).astype(F32) * 0.01, 0.0), axis=1, keepdims=True)
    steep = SHARP / rate_col

    total_m = m_all[z]
    for side in sides:
        for k in range(side[2], 0, -1):
            if next_stop(side[1], k) == 0:
                for piece in range(PIECES):
                    arrived(side, k, piece)
                total_m = total_m + side[3][k]

    h, l = split(total_m)
    g = dot(h, c_hi[...], NN) + (dot(l, c_hi[...], NN) + dot(h, c_lo[...], NN))
    const = jnp.sum(g * mean[...].reshape(1, factors), axis=1, keepdims=True) + base_col
    gh, gl = split(g)
    both = jnp.concatenate([gh.astype(F32), gl.astype(F32)], axis=0).astype(BF16)
    low_lane = lax.broadcasted_iota(jnp.int32, (8, POINTS), 1) < POINTS // 2
    for k in range(8):
        rows = pl.ds(k * POINTS, POINTS)
        first = dot(both, n_hi[rows, :], NT)
        second = dot(gh, n_lo[rows, :], NT)
        x = first[0:own_lines, :] + (first[own_lines:, :] + second) + const
        v = jnp.abs(x) * steep - SHARP
        soft = jnp.maximum(v, 0.0) + jnp.log1p(jnp.exp(-jnp.abs(v)))
        share[k : k + 1, :] = jnp.sum(soft, axis=0, keepdims=True) * (1.0 / (SHARP * lines * nl))
        top, low = x[0:8, :], x[8:16, :]
        send[2 * k] = jnp.where(low_lane, top, pltpu.roll(low, POINTS // 2, 1))
        send[2 * k + 1] = jnp.where(low_lane, pltpu.roll(top, POINTS // 2, 1), low)

    def send_to(source, slots, slot, send_sem, recv_sem, axis, peer):
        return pltpu.make_async_remote_copy(
            src_ref=source,
            dst_ref=slots.at[slot],
            send_sem=send_sem,
            recv_sem=recv_sem,
            device_id={axis: peer},
            device_id_type=MESH,
        )

    partner = pltpu.make_async_remote_copy(
        src_ref=share,
        dst_ref=pair_in,
        send_sem=cs,
        recv_sem=cr,
        device_id={"line": chip * 2 + 1 - core},
        device_id_type=MESH,
    )
    partner.start()
    recv[z] = send[z]
    partner.wait_recv()
    chip_sum[...] = share[...] + pair_in[...]

    def plane_copy(n, slot):
        peer = chip_at(*plane_order[n])
        slot = chip if slot is None else peer
        return send_to(chip_sum, plane_in, slot, ls.at[n], lr.at[slot], "line", peer * 2 + core)

    def flow_copy(d, slot):
        peer = lax.rem(z + d, nz)
        slot = z if slot is None else peer
        return send_to(send.at[peer], recv, slot, fs.at[d], fr.at[slot], "bus", peer)

    def deep_copy(d, slot):
        peer = lax.rem(z + d, nz)
        slot = z if slot is None else peer
        return send_to(plane_sum, deep_in, slot, ds.at[d], dr.at[slot], "bus", peer)

    for n in range(len(plane_order)):
        copy = plane_copy(n, None)
        copy.start()
        sent.append(copy)
    for d in z_order:
        copy = flow_copy(d, None)
        copy.start()
        sent.append(copy)
    plane_in[chip] = chip_sum[...]
    for n in range(len(plane_order)):
        plane_copy(n, n).wait_recv()
    partial = plane_in[0]
    for j in range(1, nl // 2):
        partial = partial + plane_in[j]
    plane_sum[...] = partial
    for d in z_order:
        copy = deep_copy(d, None)
        copy.start()
        sent.append(copy)
    deep_in[z] = partial

    for d in z_order:
        flow_copy(d, d).wait_recv()
    tiles = []
    for j in range(nz):
        tile = recv[j]
        tiles.append(tile)
        tiles.append(pltpu.roll(tile, POINTS // 2, 1))
    by_line = jnp.concatenate(tiles, axis=0)
    flows_o[...] = jnp.transpose(by_line)[0 : POINTS // 2, :]

    for d in z_order:
        deep_copy(d, d).wait_recv()
    total_over = deep_in[0]
    for j in range(1, nz):
        total_over = total_over + deep_in[j]
    over[...] = total_over
    emphasis = lik[...] * total_over
    total = jnp.sum(jnp.sum(emphasis, axis=1, keepdims=True), axis=0, keepdims=True)
    inverse = 1.0 / total
    flat = jnp.concatenate([emphasis[k : k + 1, :] for k in range(8)], axis=1)
    e_hi, e_lo = split(flat)
    both = jnp.concatenate(
        [e_hi.astype(F32), e_lo.astype(F32), jnp.zeros((14, flat.shape[1]), F32)], axis=0
    ).astype(BF16)
    first = dot(both, n_hi[...], NN)
    second = dot(both, n_lo[...], NN)
    moved = first[0:1, :] + (first[1:2, :] + second[0:1, :])
    newmean_o[...] = mean[...].reshape(1, factors) + moved * inverse
    row = over[pl.ds(z // 2, 1), :]
    like_row = lik[pl.ds(z // 2, 1), :]
    odd = lax.rem(z, 2) == 1
    row = jnp.where(odd, row[:, POINTS // 2 :], row[:, 0 : POINTS // 2])
    like_row = jnp.where(odd, like_row[:, POINTS // 2 :], like_row[:, 0 : POINTS // 2])
    overload_o[...] = row
    weight_o[...] = (float(8 * POINTS) * like_row) * row * inverse

    partner.wait_send()
    for copy in sent:
        copy.wait_send()


def per_device(nz, nl, ptdf, base, gain, fob, rating, dirs, shifts, chol, mean):
    lines, buses = ptdf.shape
    factors = chol.shape[0]
    half = nz // 2
    own = lines // nz
    scen = shifts.shape[0] * POINTS
    vm, dma = pltpu.VMEM, pltpu.SemaphoreType.DMA
    anywhere = pl.BlockSpec(memory_space=pl.ANY)
    inside = pl.BlockSpec(memory_space=pltpu.VMEM)
    n_loads = 10
    flows, overload, weight, new_mean = pl.pallas_call(
        functools.partial(kernel, nz, nl),
        out_shape=(
            jax.ShapeDtypeStruct((scen // nz, lines), F32),
            jax.ShapeDtypeStruct((1, scen // nz), F32),
            jax.ShapeDtypeStruct((1, scen // nz), F32),
            jax.ShapeDtypeStruct((1, factors), F32),
        ),
        in_specs=[anywhere] * 9,
        out_specs=(inside,) * 4,
        scratch_shapes=[
            vm((lines, buses), BF16),
            vm((buses,), F32),
            vm((buses,), F32),
            vm((buses,), jnp.int32),
            vm((lines,), jnp.int32),
            vm(dirs.shape, jnp.int32),
            vm(shifts.shape, jnp.int32),
            vm(chol.shape, F32),
            vm((factors,), F32),
            vm((nz, own, factors), F32),
            vm((half + 1, own, factors), F32),
            vm((half, own, factors), F32),
            vm((POINTS, factors), jnp.int32),
            vm((scen, factors), BF16),
            vm((scen, factors), BF16),
            vm(chol.shape, BF16),
            vm(chol.shape, BF16),
            vm((8, POINTS), F32),
            vm((2, POINTS), F32),
            vm((nz, 2, POINTS), F32),
            vm((nz, 8, POINTS), F32),
            vm((nz, 8, POINTS), F32),
            vm((8, POINTS), F32),
            vm((8, POINTS), F32),
            vm((8, POINTS), F32),
            vm((nl // 2, 8, POINTS), F32),
            vm((8, POINTS), F32),
            vm((nz, 8, POINTS), F32),
            vm((8, POINTS), F32),
            dma((n_loads,)),
            dma((half + 1, PIECES)),
            dma((half + 1, PIECES)),
            dma((half, PIECES)),
            dma((half, PIECES)),
            dma((nz,)),
            dma((nz,)),
            dma((nz,)),
            dma((nz,)),
            dma(()),
            dma(()),
            dma((nl // 2,)),
            dma((nl // 2,)),
            dma((nz,)),
            dma((nz,)),
        ],
        compiler_params=pltpu.CompilerParams(
            collective_id=0, has_side_effects=True, vmem_limit_bytes=40 * 1024 * 1024
        ),
    )(
        *[
            pltpu.with_memory_space_constraint(a, pltpu.HBM)
            for a in (ptdf, base, gain, fob, rating, dirs, shifts, chol, mean)
        ]
    )
    return flows, overload.reshape(-1), weight.reshape(-1), new_mean.reshape(-1)


def solution(mesh):
    nz, nl = mesh.shape["bus"], mesh.shape["line"]
    return jax.shard_map(
        functools.partial(per_device, nz, nl),
        mesh=mesh,
        in_specs=(P("line", "bus"), P("bus"), P("bus"), P("bus"), P("line"), P(), P(), P(), P()),
        out_specs=(P("bus", "line"), P("bus"), P("bus"), P()),
        check_vma=False,
    )
```

time: 70.6 us -> 52.3 us (0.74)
  Pallas kernels: 58.8 us -> 49.3 us
  local copies, waits for them, and re-layouts: 10.6 us -> 2.23 us
    pallas_call x1, Pallas kernels: 58.8 us -> 49.3 us  [per_device(): pl.pallas_call(functools.partial(kernel, nz, nl), out_shape=(jax.ShapeDty...]
    unnamed x16 -> x4, local copies, waits for them, and re-layouts: 8.28 us -> 2.23 us
    reshape x3 -> x0, local copies, waits for them, and re-layouts: 2.3 us -> none  [the longest x1 0.77 us: per_device(): gain.reshape(1, buses)]
where the time goes in v2:
time: 52.3 us; the launch traced here: 52.2 us
  Pallas kernels  49.3 us (94%)
  local copies, waits for them, and re-layouts  2.23 us (4%)
  between operations  0.64 us (1%)
    pallas_call x1, Pallas kernels, per_device(): pl.pallas_call(functools.partial(kernel, nz, nl), out_shape=(jax.ShapeDty...  49.3 us
    unnamed x4, local copies, waits for them, and re-layouts  2.23 us

profile of v2, /device:TPU:1, one launch (start us, length us, event | category | flops | bytes accessed | tf_op | source)
XLA Modules:
  0.0 52.2 jit_solution(14080272576645743411)
XLA Ops:
  0.6 49.3 %shard_map.120 = (f32[64,256]{1,0:T(8,128)S(1)}, f32[1,64]{1,0:T(1,128)S(1)}, f32[1,64]{1,0:T(1,128)S(1)}, f32[1,512]{1,0:T(1,128)S(1)}) custom-call(bf16[256,6272]{1,0:T(8,128)(2,1)} %ptdf_h.1, f32[6272]{0:T(1024)} %base_h.1, f32[6272]{0:T(1024)} %gain_h.1, s32[6272]{0:T(1024)} %fob_h.1, s32[256]{0:T(256)} %rating_h.1, s32[30,512]{1,0:T(8,128)} %dirs_h.1, ...), custom_call_target="tpu_custom_call" | custom-call | tf_op jit(solution)/shard_map/pallas_call | solution.py:482
  49.9 0.6 %copy.17 = f32[64,256]{1,0:T(8,128)} copy(f32[64,256]{1,0:T(8,128)S(1)} %get-tuple-element.16) | data formatting | bytes 131072
  50.6 0.5 copy.18
  51.1 0.5 copy.19
  51.6 0.6 %copy.20 = f32[512]{0:T(512)} copy(f32[512]{0:T(512)S(1)} %bitcast.3) | data formatting | bytes 4096

commit v3 on v2

--- a/solution.py
+++ b/solution.py
@@ -15,10 +15,11 @@
 BF16 = jnp.bfloat16
 NT = (((1,), (1,)), ((), ()))
 NN = (((1,), (0,)), ((), ()))
-PIECES = 2
-PLUS = (6, 3, 0)
-MINUS = (5, 2, 0)
-GAPS = ((0, 1, 2), (3, 4, 5), (6, 7))
+WIDTHS = (256, 256)
+PIECES = len(WIDTHS)
+LONG = (6, 3, 0)
+SHORT = (5, 2, 0)
+GAPS = ((0, 1), (2, 3, 4), (5, 6, 7))
 
 CENTRAL = (
     2.81022636e-08,
@@ -99,8 +100,7 @@
     chol,
     mean,
     m_all,
-    ring_p,
-    ring_m,
+    ring,
     table,
     n_hi,
     n_lo,
@@ -119,12 +119,8 @@
     deep_in,
     over,
     load_sem,
-    ps,
-    pr,
-    ms,
-    mr,
-    bs,
-    br,
+    ring_s,
+    ring_r,
     fs,
     fr,
     cs,
@@ -167,13 +163,11 @@
 
     barrier = pltpu.get_barrier_semaphore()
 
-    def greet_z(d, carry):
-        pl.semaphore_signal(
-            barrier, inc=1, device_id={"bus": lax.rem(z + d, nz)}, device_id_type=MESH
-        )
-        return carry
-
-    lax.fori_loop(1, nz, greet_z, 0)
+    reach = max(a - b for a, b in zip((half,) + LONG, LONG + (0,)))
+    reach = max(reach, 3)
+    for d in range(1, reach + 1):
+        for peer in (lax.rem(z + d, nz), lax.rem(z + nz - d, nz)):
+            pl.semaphore_signal(barrier, inc=1, device_id={"bus": peer}, device_id_type=MESH)
     for i, j in plane_order:
         pl.semaphore_signal(
             barrier,
@@ -185,24 +179,37 @@
         barrier, inc=1, device_id={"line": chip * 2 + 1 - core}, device_id_type=MESH
     )
 
-    wide = factors // PIECES
-
-    factor = lax.broadcasted_iota(jnp.int32, (wide, 128), 0).astype(F32).astype(BF16)
-    nothing = jnp.zeros((wide, 128), BF16)
+    starts = [sum(WIDTHS[:p]) for p in range(PIECES)]
+
+    def lanes(piece):
+        return pl.ds(starts[piece], WIDTHS[piece])
+
+    def columns(height):
+        return lax.broadcasted_iota(jnp.int32, (height, 128), 0).astype(F32).astype(BF16)
+
+    def spread(value, j, height):
+        return jnp.broadcast_to(value[:, j : j + 128], (height, 128))
 
     def gather(piece):
-        acc = None
+        acc, wide = None, WIDTHS[piece]
         for i, (k, size) in enumerate(blocks):
+            g_hi, g_lo = split(gain[pl.ds(k, size)].reshape(1, size))
+            hi, lo = [], []
+            for offset in range(0, wide, 256):
+                height = min(256, wide - offset)
+                nothing = jnp.zeros((height, 128), BF16)
+                which = fob[pl.ds(k, size)].reshape(1, size) - (starts[piece] + offset)
+                which = which.astype(F32).astype(BF16)
+                hits = [columns(height) == spread(which, j, height) for j in range(0, size, 128)]
+                for terms, value in ((hi, g_hi), (lo, g_lo)):
+                    row = [
+                        jnp.where(hits[j // 128], spread(value, j, height), nothing)
+                        for j in range(0, size, 128)
+                    ]
+                    terms.append(jnp.concatenate(row, axis=1))
+            stack = hi + lo
             if piece == 0:
                 loads[len(first) + i].wait()
-            g_hi, g_lo = split(gain[pl.ds(k, size)].reshape(1, size))
-            which = (fob[pl.ds(k, size)].reshape(1, size) - wide * piece).astype(F32).astype(BF16)
-            hi, lo = [], []
-            for j in range(0, size, 128):
-                hit = factor == jnp.broadcast_to(which[:, j : j + 128], (wide, 128))
-                hi.append(jnp.where(hit, jnp.broadcast_to(g_hi[:, j : j + 128], (wide, 128)), nothing))
-                lo.append(jnp.where(hit, jnp.broadcast_to(g_lo[:, j : j + 128], (wide, 128)), nothing))
-            stack = [jnp.concatenate(hi, axis=1), jnp.concatenate(lo, axis=1)]
             if piece == 0:
                 b_hi, b_lo = split(base[pl.ds(k, size)].reshape(1, size))
                 stack.append(
@@ -213,63 +220,88 @@
             part = dot(jnp.concatenate(stack, axis=0), ptdf[:, pl.ds(k, size)], NT)
             acc = part if acc is None else acc + part
         by_line = jnp.transpose(acc[0:wide] + acc[wide : 2 * wide])
-        m_all[:, :, wide * piece : wide * (piece + 1)] = by_line.reshape(nz, lines // nz, wide)
+        m_all[:, :, lanes(piece)] = by_line.reshape(nz, lines // nz, wide)
         if piece == 0:
             total_row = acc[2 * wide : 2 * wide + 1] + acc[2 * wide + 1 : 2 * wide + 2]
-            base_row[0:1, :] = total_row[:, 0 : lines // 2]
-            base_row[1:2, :] = total_row[:, lines // 2 :]
-
-    def lanes(piece):
-        return pl.ds(piece * wide, wide)
-
-    sides = (
-        (1, PLUS, half, ring_p, ps, pr),
-        (-1, MINUS, half - 1, ring_m, ms, mr),
+            base_row[0] = total_row[:, 0 : lines // 2]
+            base_row[1] = total_row[:, lines // 2 :]
+
+    def piece_of(piece, long_sign, start, land):
+        sides = (
+            (long_sign, LONG, half, 0 if long_sign > 0 else 1),
+            (-long_sign, SHORT, half - 1, 0 if long_sign < 0 else 1),
+        )
+        return piece, sides, start, land
+
+    pieces = [
+        piece_of(
+            p,
+            1 if p == 0 else -1,
+            lambda d, p=p: m_all.at[d, :, lanes(p)],
+            lambda way, k, p=p: ring.at[way, k, :, lanes(p)],
+        )
+        for p in range(PIECES)
+    ]
+    pieces.append(
+        piece_of(
+            PIECES, -1, lambda d: base_row.at[d // (nz // 2)], lambda way, k: base_in.at[way, k]
+        )
     )
 
     def toward(sign, k):
         return lax.rem(z + sign * k + nz, nz)
 
-    def hop(side, k, piece, source):
-        sign, stops, far, ring, send_sem, recv_sem = side
+    def hop(piece, side, k, source):
+        index, _, _, land = piece
+        sign, stops, _, way = side
         return pltpu.make_async_remote_copy(
             src_ref=source,
-            dst_ref=ring.at[k, :, lanes(piece)],
-            send_sem=send_sem.at[k, piece],
-            recv_sem=recv_sem.at[k, piece],
+            dst_ref=land(way, k),
+            send_sem=ring_s.at[index, way, k],
+            recv_sem=ring_r.at[index, way, k],
             device_id={"bus": toward(sign, k - next_stop(stops, k))},
             device_id_type=MESH,
         )
 
-    def arrived(side, k, piece):
-        hop(side, k, piece, side[3].at[k, :, lanes(piece)]).wait_recv()
+    def arrived(piece, side, k):
+        hop(piece, side, k, piece[3](side[3], k)).wait_recv()
 
     sent = []
 
-    def direct(piece):
-        far = max(side[2] for side in sides)
-        for k in range(far, 0, -1):
+    def direct(piece, level):
+        _, sides, start, _ = piece
+        for k in range(half, 0, -1):
             for side in sides:
-                if k <= side[2] and k not in side[1]:
-                    copy = hop(side, k, piece, m_all.at[toward(side[0], k), :, lanes(piece)])
+                sign, stops, far, _ = side
+                if k <= far and k not in stops and next_stop(stops, k) == stops[level]:
+                    copy = hop(piece, side, k, start(toward(sign, k)))
                     copy.start()
                     sent.append(copy)
 
-    def merge(level, piece):
+    def merge(piece, level):
+        _, sides, start, land = piece
         for side in sides:
-            sign, stops, far, ring, _, _ = side
-            if level >= len(stops) - 1:
-                continue
+            sign, stops, far, way = side
             c = stops[level]
             members = [k for k in range(far, 0, -1) if next_stop(stops, k) == c]
-            block = m_all[toward(sign, c), :, lanes(piece)]
+            block = start(toward(sign, c))[...]
             for k in members:
-                arrived(side, k, piece)
-                block = block + ring[k, :, lanes(piece)]
-            ring[members[0], :, lanes(piece)] = block
-            copy = hop(side, c, piece, ring.at[members[0], :, lanes(piece)])
+                arrived(piece, side, k)
+                block = block + land(way, k)[...]
+            land(way, members[0])[...] = block
+            copy = hop(piece, side, c, land(way, members[0]))
             copy.start()
             sent.append(copy)
+
+    def collect(piece):
+        _, sides, start, land = piece
+        block = start(z)[...]
+        for side in sides:
+            for k in range(side[2], 0, -1):
+                if next_stop(side[1], k) == 0:
+                    arrived(piece, side, k)
+                    block = block + land(side[3], k)[...]
+        return block
 
     def prepare():
         for copy in loads[len(first) + len(blocks) :]:
@@ -298,44 +330,31 @@
         second = dot(both, lo, NT)
         lik[t : t + 1, :] = jnp.exp(-(first[0:1, :] + (first[1:2, :] + second[0:1, :])))
 
-    def base_copy(d, slot):
-        return pltpu.make_async_remote_copy(
-            src_ref=base_row,
-            dst_ref=base_in.at[slot],
-            send_sem=bs.at[d],
-            recv_sem=br.at[slot],
-            device_id={"bus": lax.rem(z + d, nz)},
-            device_id_type=MESH,
-        )
-
     for copy in loads[: len(first)]:
         copy.wait()
     gather(0)
-    pl.semaphore_wait(barrier, nz + nl // 2 - 1)
-    direct(0)
-    for d in z_order:
-        copy = base_copy(d, z)
-        copy.start()
-        sent.append(copy)
-    base_in[z] = base_row[...]
-    for piece in range(1, PIECES):
-        gather(piece)
-        direct(piece)
+    pl.semaphore_wait(barrier, 2 * reach + nl // 2)
+    direct(pieces[0], 0)
+    direct(pieces[PIECES], 0)
+    direct(pieces[0], 1)
+    gather(1)
+    direct(pieces[1], 0)
+    direct(pieces[1], 1)
+    direct(pieces[PIECES], 1)
     prepare()
-    for level in range(len(PLUS)):
+    for level in range(len(LONG)):
         for t in GAPS[level]:
             shadow(t)
-        if level < len(PLUS) - 1:
-            for piece in range(PIECES):
-                merge(level, piece)
-
-    for d in z_order:
-        base_copy(d, lax.rem(z + d, nz)).wait_recv()
+        if level < len(LONG) - 1:
+            for piece in pieces:
+                merge(piece, level)
+        if level == 0:
+            for piece in pieces:
+                direct(piece, 2)
+
     own_lines = lines // nz
-    base_sum = base_in[0]
-    for j in range(1, nz):
-        base_sum = base_sum + base_in[j]
-    base_line = jnp.concatenate([base_sum[0:1, :], base_sum[1:2, :]], axis=1)
+    base_line = collect(pieces[PIECES])
+    base_line = jnp.concatenate([base_line, base_line], axis=1)
     mine = lax.broadcasted_iota(jnp.int32, (own_lines, lines), 1) == (
         lax.broadcasted_iota(jnp.int32, (own_lines, lines), 0) + z * own_lines
     )
@@ -343,13 +362,7 @@
     rate_col = jnp.sum(jnp.where(mine, rating[...].reshape(1, lines).astype(F32) * 0.01, 0.0), axis=1, keepdims=True)
     steep = SHARP / rate_col
 
-    total_m = m_all[z]
-    for side in sides:
-        for k in range(side[2], 0, -1):
-            if next_stop(side[1], k) == 0:
-                for piece in range(PIECES):
-                    arrived(side, k, piece)
-                total_m = total_m + side[3][k]
+    total_m = jnp.concatenate([collect(pieces[p]) for p in range(PIECES)], axis=1)
 
     h, l = split(total_m)
     g = dot(h, c_hi[...], NN) + (dot(l, c_hi[...], NN) + dot(h, c_lo[...], NN))
@@ -467,6 +480,19 @@
     partner.wait_send()
     for copy in sent:
         copy.wait_send()
+
+
+def deliver(*refs):
+    sources, targets, sem = refs[0:4], refs[4:8], refs[8]
+    copies = []
+    for i, (source, target) in enumerate(zip(sources, targets)):
+        if len(target.shape) == 1:
+            source = source.at[0]
+        copies.append(pltpu.make_async_copy(source, target, sem.at[i]))
+    for copy in copies:
+        copy.start()
+    for copy in copies:
+        copy.wait()
 
 
 def per_device(nz, nl, ptdf, base, gain, fob, rating, dirs, shifts, chol, mean):
@@ -500,16 +526,15 @@
             vm(chol.shape, F32),
             vm((factors,), F32),
             vm((nz, own, factors), F32),
-            vm((half + 1, own, factors), F32),
-            vm((half, own, factors), F32),
+            vm((2, half + 1, own, factors), F32),
             vm((POINTS, factors), jnp.int32),
             vm((scen, factors), BF16),
             vm((scen, factors), BF16),
             vm(chol.shape, BF16),
             vm(chol.shape, BF16),
             vm((8, POINTS), F32),
-            vm((2, POINTS), F32),
-            vm((nz, 2, POINTS), F32),
+            vm((2, 1, POINTS), F32),
+            vm((2, half + 1, 1, POINTS), F32),
             vm((nz, 8, POINTS), F32),
             vm((nz, 8, POINTS), F32),
             vm((8, POINTS), F32),
@@ -520,12 +545,8 @@
             vm((nz, 8, POINTS), F32),
             vm((8, POINTS), F32),
             dma((n_loads,)),
-            dma((half + 1, PIECES)),
-            dma((half + 1, PIECES)),
-            dma((half, PIECES)),
-            dma((half, PIECES)),
-            dma((nz,)),
-            dma((nz,)),
+            dma((PIECES + 1, 2, half + 1)),
+            dma((PIECES + 1, 2, half + 1)),
             dma((nz,)),
             dma((nz,)),
             dma(()),
@@ -544,7 +565,15 @@
             for a in (ptdf, base, gain, fob, rating, dirs, shifts, chol, mean)
         ]
     )
-    return flows, overload.reshape(-1), weight.reshape(-1), new_mean.reshape(-1)
+    results = (flows, overload, weight, new_mean)
+    return pl.pallas_call(
+        deliver,
+        out_shape=tuple(jax.ShapeDtypeStruct(a.shape if a.shape[0] > 1 else a.shape[1:], F32) for a in results),
+        in_specs=[pl.BlockSpec(memory_space=pltpu.VMEM)] * 4,
+        out_specs=(anywhere,) * 4,
+        scratch_shapes=[dma((4,))],
+        compiler_params=pltpu.CompilerParams(vmem_limit_bytes=1024 * 1024),
+    )(*results)
 
 
 def solution(mesh):

time: 52.3 us -> 50.6 us (0.967)
  local copies, waits for them, and re-layouts: 2.23 us -> 0 us
  Pallas kernels: 49.3 us -> 49.9 us
    unnamed x4 -> x0, local copies, waits for them, and re-layouts: 2.23 us -> none
    pallas_call x0 -> x1, Pallas kernels: none -> 0.67 us  [per_device(): pl.pallas_call(deliver, out_shape=tuple((jax.ShapeDtypeStruct(a.shape if...]
where the time goes in v3:
time: 50.6 us; the launch traced here: 50.5 us
  Pallas kernels  49.9 us (99%)
  between operations  0.64 us (1%)
    pallas_call x1, Pallas kernels, per_device(): pl.pallas_call(functools.partial(kernel, nz, nl), out_shape=(jax.ShapeDty...  49.2 us

profile of v3, /device:TPU:1, one launch (start us, length us, event | category | flops | bytes accessed | tf_op | source)
XLA Modules:
  0.0 50.5 jit_solution(3802928239553285332)
XLA Ops:
  0.6 49.2 %shard_map.120 = (f32[64,256]{1,0:T(8,128)S(1)}, f32[1,64]{1,0:T(1,128)S(1)}, f32[1,64]{1,0:T(1,128)S(1)}, f32[1,512]{1,0:T(1,128)S(1)}) custom-call(bf16[256,6272]{1,0:T(8,128)(2,1)} %ptdf_h.1, f32[6272]{0:T(1024)} %base_h.1, f32[6272]{0:T(1024)} %gain_h.1, s32[6272]{0:T(1024)} %fob_h.1, s32[256]{0:T(256)} %rating_h.1, s32[30,512]{1,0:T(8,128)} %dirs_h.1, ...), custom_call_target="tpu_custom_call" | custom-call | tf_op jit(solution)/shard_map/pallas_call | solution.py:508
  49.8 0.7 %shard_map.121 = (f32[64,256]{1,0:T(8,128)}, f32[64]{0:T(128)}, f32[64]{0:T(128)}, f32[512]{0:T(512)}) custom-call(f32[64,256]{1,0:T(8,128)S(1)} %get-tuple-element.8.refs_0_, f32[1,64]{1,0:T(1,128)S(1)} %get-tuple-element.9.refs_1_, f32[1,64]{1,0:T(1,128)S(1)} %get-tuple-element.10.refs_2_, f32[1,512]{1,0:T(1,128)S(1)} %get-tuple-element.11.refs_3_), custom_call_target="tpu_custom_call" | custom-call | tf_op jit(solution)/shard_map/pallas_call | solution.py:569

commit v4 on v3

--- a/solution.py
+++ b/solution.py
@@ -17,9 +17,10 @@
 NN = (((1,), (0,)), ((), ()))
 WIDTHS = (256, 256)
 PIECES = len(WIDTHS)
+BLOCK = 3072
 LONG = (6, 3, 0)
 SHORT = (5, 2, 0)
-GAPS = ((0, 1), (2, 3, 4), (5, 6, 7))
+GAPS = ((0, 2), (2, 5), (5, 8))
 
 CENTRAL = (
     2.81022636e-08,
@@ -100,6 +101,7 @@
     chol,
     mean,
     m_all,
+    totals,
     ring,
     table,
     n_hi,
@@ -135,8 +137,9 @@
     lines, buses = ptdf.shape
     factors = chol.shape[0]
     half = nz // 2
-    cut = buses // 2 // 128 * 128 + 128
-    blocks = [(0, cut), (cut, buses - cut)]
+    full = buses // BLOCK
+    rest = buses - full * BLOCK
+    blocks = [(k, min(BLOCK, buses - k)) for k in range(0, buses, BLOCK)]
     chip, core = me // 2, lax.rem(me, 2)
     row_of, col_of = chip // 4, lax.rem(chip, 4)
     z_order = [d for (d,) in far_first([(d,) for d in range(1, nz)], (nz,))]
@@ -191,25 +194,21 @@
         return jnp.broadcast_to(value[:, j : j + 128], (height, 128))
 
     def gather(piece):
-        acc, wide = None, WIDTHS[piece]
-        for i, (k, size) in enumerate(blocks):
+        wide = WIDTHS[piece]
+        height = 2 * wide + (16 if piece == 0 else 0)
+        nothing = jnp.zeros((wide, 128), BF16)
+
+        def product(k, size, index):
             g_hi, g_lo = split(gain[pl.ds(k, size)].reshape(1, size))
-            hi, lo = [], []
-            for offset in range(0, wide, 256):
-                height = min(256, wide - offset)
-                nothing = jnp.zeros((height, 128), BF16)
-                which = fob[pl.ds(k, size)].reshape(1, size) - (starts[piece] + offset)
-                which = which.astype(F32).astype(BF16)
-                hits = [columns(height) == spread(which, j, height) for j in range(0, size, 128)]
-                for terms, value in ((hi, g_hi), (lo, g_lo)):
-                    row = [
-                        jnp.where(hits[j // 128], spread(value, j, height), nothing)
-                        for j in range(0, size, 128)
-                    ]
-                    terms.append(jnp.concatenate(row, axis=1))
-            stack = hi + lo
-            if piece == 0:
-                loads[len(first) + i].wait()
+            which = (fob[pl.ds(k, size)].reshape(1, size) - starts[piece]).astype(F32).astype(BF16)
+            hits = [columns(wide) == spread(which, j, wide) for j in range(0, size, 128)]
+            stack = []
+            for value in (g_hi, g_lo):
+                row = [
+                    jnp.where(hits[j // 128], spread(value, j, wide), nothing)
+                    for j in range(0, size, 128)
+                ]
+                stack.append(jnp.concatenate(row, axis=1))
             if piece == 0:
                 b_hi, b_lo = split(base[pl.ds(k, size)].reshape(1, size))
                 stack.append(
@@ -217,8 +216,22 @@
                         [b_hi.astype(F32), b_lo.astype(F32), jnp.zeros((14, size), F32)], axis=0
                     ).astype(BF16)
                 )
-            part = dot(jnp.concatenate(stack, axis=0), ptdf[:, pl.ds(k, size)], NT)
-            acc = part if acc is None else acc + part
+                pltpu.make_async_copy(
+                    ptdf_h.at[:, pl.ds(k, size)],
+                    ptdf.at[:, pl.ds(k, size)],
+                    load_sem.at[len(first) + index],
+                ).wait()
+            return dot(jnp.concatenate(stack, axis=0), ptdf[:, pl.ds(k, size)], NT)
+
+        def step(i, carry):
+            totals[0:height] += product(pl.multiple_of(i * BLOCK, BLOCK), BLOCK, i)
+            return carry
+
+        totals[0:height] = jnp.zeros((height, lines), F32)
+        lax.fori_loop(0, full, step, 0)
+        acc = totals[0:height]
+        if rest:
+            acc = acc + product(full * BLOCK, rest, full)
         by_line = jnp.transpose(acc[0:wide] + acc[wide : 2 * wide])
         m_all[:, :, lanes(piece)] = by_line.reshape(nz, lines // nz, wide)
         if piece == 0:
@@ -316,9 +329,9 @@
         c_hi[...] = hi
         c_lo[...] = lo
 
-    def shadow(t):
-        rows = pl.ds(t * POINTS, POINTS)
-        normal = draw(table[...] ^ shifts[t : t + 1, :])
+    def shadow(t, carry):
+        rows = pl.ds(pl.multiple_of(t * POINTS, POINTS), POINTS)
+        normal = draw(table[...] ^ shifts[pl.ds(t, 1), :])
         hi, lo = split(normal)
         n_hi[rows, :] = hi
         n_lo[rows, :] = lo
@@ -328,7 +341,8 @@
         ).astype(BF16)
         first = dot(both, hi, NT)
         second = dot(both, lo, NT)
-        lik[t : t + 1, :] = jnp.exp(-(first[0:1, :] + (first[1:2, :] + second[0:1, :])))
+        lik[pl.ds(t, 1), :] = jnp.exp(-(first[0:1, :] + (first[1:2, :] + second[0:1, :])))
+        return carry
 
     for copy in loads[: len(first)]:
         copy.wait()
@@ -343,8 +357,7 @@
     direct(pieces[PIECES], 1)
     prepare()
     for level in range(len(LONG)):
-        for t in GAPS[level]:
-            shadow(t)
+        lax.fori_loop(GAPS[level][0], GAPS[level][1], shadow, 0)
         if level < len(LONG) - 1:
             for piece in pieces:
                 merge(piece, level)
@@ -504,7 +517,7 @@
     vm, dma = pltpu.VMEM, pltpu.SemaphoreType.DMA
     anywhere = pl.BlockSpec(memory_space=pl.ANY)
     inside = pl.BlockSpec(memory_space=pltpu.VMEM)
-    n_loads = 10
+    n_loads = 8 + -(-buses // BLOCK)
     flows, overload, weight, new_mean = pl.pallas_call(
         functools.partial(kernel, nz, nl),
         out_shape=(
@@ -526,6 +539,7 @@
             vm(chol.shape, F32),
             vm((factors,), F32),
             vm((nz, own, factors), F32),
+            vm((2 * max(WIDTHS) + 16, lines), F32),
             vm((2, half + 1, own, factors), F32),
             vm((POINTS, factors), jnp.int32),
             vm((scen, factors), BF16),

time: 50.6 us -> 48.2 us (0.953)
  Pallas kernels: 49.9 us -> 47.4 us
    pallas_call x1, Pallas kernels: 49.2 us -> 46.8 us  [per_device(): pl.pallas_call(functools.partial(kernel, nz, nl), out_shape=(jax.ShapeDty...]
where the time goes in v4:
time: 48.2 us; the launch traced here: 48.1 us
  Pallas kernels  47.4 us (98%)
  between operations  0.64 us (1%)
    pallas_call x1, Pallas kernels, per_device(): pl.pallas_call(functools.partial(kernel, nz, nl), out_shape=(jax.ShapeDty...  46.8 us

profile of v4, /device:TPU:1, one launch (start us, length us, event | category | flops | bytes accessed | tf_op | source)
XLA Modules:
  0.0 48.1 jit_solution(461988457381436154)
XLA Ops:
  0.6 46.8 %shard_map.120 = (f32[64,256]{1,0:T(8,128)S(1)}, f32[1,64]{1,0:T(1,128)S(1)}, f32[1,64]{1,0:T(1,128)S(1)}, f32[1,512]{1,0:T(1,128)S(1)}) custom-call(bf16[256,6272]{1,0:T(8,128)(2,1)} %ptdf_h.1, f32[6272]{0:T(1024)} %base_h.1, f32[6272]{0:T(1024)} %gain_h.1, s32[6272]{0:T(1024)} %fob_h.1, s32[256]{0:T(256)} %rating_h.1, s32[30,512]{1,0:T(8,128)} %dirs_h.1, ...), custom_call_target="tpu_custom_call" | custom-call | tf_op jit(solution)/shard_map/pallas_call | solution.py:521
  47.4 0.7 %shard_map.121 = (f32[64,256]{1,0:T(8,128)}, f32[64]{0:T(128)}, f32[64]{0:T(128)}, f32[512]{0:T(512)}) custom-call(f32[64,256]{1,0:T(8,128)S(1)} %get-tuple-element.8.refs_0_, f32[1,64]{1,0:T(1,128)S(1)} %get-tuple-element.9.refs_1_, f32[1,64]{1,0:T(1,128)S(1)} %get-tuple-element.10.refs_2_, f32[1,512]{1,0:T(1,128)S(1)} %get-tuple-element.11.refs_3_), custom_call_target="tpu_custom_call" | custom-call | tf_op jit(solution)/shard_map/pallas_call | solution.py:583

commit v5 on v4

--- a/solution.py
+++ b/solution.py
@@ -17,7 +17,7 @@
 NN = (((1,), (0,)), ((), ()))
 WIDTHS = (256, 256)
 PIECES = len(WIDTHS)
-BLOCK = 3072
+BLOCK = 3200
 LONG = (6, 3, 0)
 SHORT = (5, 2, 0)
 GAPS = ((0, 2), (2, 5), (5, 8))
@@ -137,9 +137,10 @@
     lines, buses = ptdf.shape
     factors = chol.shape[0]
     half = nz // 2
-    full = buses // BLOCK
-    rest = buses - full * BLOCK
-    blocks = [(k, min(BLOCK, buses - k)) for k in range(0, buses, BLOCK)]
+    full = -(-buses // BLOCK)
+    overlap = full * BLOCK - buses
+    stride = BLOCK - overlap
+    blocks = [(0, BLOCK), (BLOCK, buses - BLOCK)]
     chip, core = me // 2, lax.rem(me, 2)
     row_of, col_of = chip // 4, lax.rem(chip, 4)
     z_order = [d for (d,) in far_first([(d,) for d in range(1, nz)], (nz,))]
@@ -199,8 +200,10 @@
         nothing = jnp.zeros((wide, 128), BF16)
 
         def product(k, size, index):
+            fresh = (lax.broadcasted_iota(jnp.int32, (1, size), 1) >= overlap) | (index == 0)
             g_hi, g_lo = split(gain[pl.ds(k, size)].reshape(1, size))
-            which = (fob[pl.ds(k, size)].reshape(1, size) - starts[piece]).astype(F32).astype(BF16)
+            which = jnp.where(fresh, fob[pl.ds(k, size)].reshape(1, size) - starts[piece], -1)
+            which = which.astype(F32).astype(BF16)
             hits = [columns(wide) == spread(which, j, wide) for j in range(0, size, 128)]
             stack = []
             for value in (g_hi, g_lo):
@@ -210,28 +213,23 @@
                 ]
                 stack.append(jnp.concatenate(row, axis=1))
             if piece == 0:
-                b_hi, b_lo = split(base[pl.ds(k, size)].reshape(1, size))
+                b_hi, b_lo = split(jnp.where(fresh, base[pl.ds(k, size)].reshape(1, size), 0.0))
                 stack.append(
                     jnp.concatenate(
                         [b_hi.astype(F32), b_lo.astype(F32), jnp.zeros((14, size), F32)], axis=0
                     ).astype(BF16)
                 )
-                pltpu.make_async_copy(
-                    ptdf_h.at[:, pl.ds(k, size)],
-                    ptdf.at[:, pl.ds(k, size)],
-                    load_sem.at[len(first) + index],
-                ).wait()
+                for i, (start, length) in enumerate(blocks):
+                    pl.when(index == i)(loads[len(first) + i].wait)
             return dot(jnp.concatenate(stack, axis=0), ptdf[:, pl.ds(k, size)], NT)
 
         def step(i, carry):
-            totals[0:height] += product(pl.multiple_of(i * BLOCK, BLOCK), BLOCK, i)
+            totals[0:height] += product(pl.multiple_of(i * stride, 128), BLOCK, i)
             return carry
 
         totals[0:height] = jnp.zeros((height, lines), F32)
         lax.fori_loop(0, full, step, 0)
         acc = totals[0:height]
-        if rest:
-            acc = acc + product(full * BLOCK, rest, full)
         by_line = jnp.transpose(acc[0:wide] + acc[wide : 2 * wide])
         m_all[:, :, lanes(piece)] = by_line.reshape(nz, lines // nz, wide)
         if piece == 0:

time: 48.2 us -> 48.2 us (level)
  no operation moved by 1% of the time
where the time goes in v5:
time: 48.2 us; the launch traced here: 48 us
  Pallas kernels  47.4 us (98%)
  between operations  0.64 us (1%)
    pallas_call x1, Pallas kernels, per_device(): pl.pallas_call(functools.partial(kernel, nz, nl), out_shape=(jax.ShapeDty...  46.7 us

profile of v5, /device:TPU:1, one launch (start us, length us, event | category | flops | bytes accessed | tf_op | source)
XLA Modules:
  0.0 48.0 jit_solution(9936690592159853974)
XLA Ops:
  0.6 46.7 %shard_map.120 = (f32[64,256]{1,0:T(8,128)S(1)}, f32[1,64]{1,0:T(1,128)S(1)}, f32[1,64]{1,0:T(1,128)S(1)}, f32[1,512]{1,0:T(1,128)S(1)}) custom-call(bf16[256,6272]{1,0:T(8,128)(2,1)} %ptdf_h.1, f32[6272]{0:T(1024)} %base_h.1, f32[6272]{0:T(1024)} %gain_h.1, s32[6272]{0:T(1024)} %fob_h.1, s32[256]{0:T(256)} %rating_h.1, s32[30,512]{1,0:T(8,128)} %dirs_h.1, ...), custom_call_target="tpu_custom_call" | custom-call | tf_op jit(solution)/shard_map/pallas_call | solution.py:519
  47.4 0.7 %shard_map.121 = (f32[64,256]{1,0:T(8,128)}, f32[64]{0:T(128)}, f32[64]{0:T(128)}, f32[512]{0:T(512)}) custom-call(f32[64,256]{1,0:T(8,128)S(1)} %get-tuple-element.8.refs_0_, f32[1,64]{1,0:T(1,128)S(1)} %get-tuple-element.9.refs_1_, f32[1,64]{1,0:T(1,128)S(1)} %get-tuple-element.10.refs_2_, f32[1,512]{1,0:T(1,128)S(1)} %get-tuple-element.11.refs_3_), custom_call_target="tpu_custom_call" | custom-call | tf_op jit(solution)/shard_map/pallas_call | solution.py:581
